TPU v7x, 256 devices: a whole 4x4x8 slice. The times are simulated.
256 devices in a mesh: fsdp: 8 (over x, core), ctx: 32 (over y, z).
Axes of the slice: x: 4, y: 4, z: 8, core: 2. Of those that a mesh axis runs over, the one named last changes fastest.
Arguments:
- hidden: bfloat16 [8, 4096, 2304], P('fsdp', 'ctx'), may hold values from -6 to 6
- query_heads: bfloat16 [8, 4096, 2048], P('fsdp', 'ctx'), may hold values from -6 to 6
- key_heads: bfloat16 [8, 4096, 2048], P('fsdp', 'ctx'), may hold values from -6 to 6
- value_heads: bfloat16 [8, 4096, 2048], P('fsdp', 'ctx'), may hold values from -6 to 6
- out_grad: bfloat16 [8, 4096, 2048], P('fsdp', 'ctx'), may hold values from -6 to 6
- checkpoint: float32 [8, 32, 16, 128, 128], P('fsdp', 'ctx'), may hold values from -6 to 6
- gate_down: bfloat16 [2304, 128], P('fsdp'), may hold values from -0.125 to 0.125
- gate_up: bfloat16 [128, 2048], P(None, 'fsdp'), may hold values from -0.5 to 0.5
- gate_bias: float32 [2048], replicated, may hold values from -4 to 4
- decay_rate: float32 [2048], replicated, may hold values from 4.8828126e-05 to 0.05
- beta_weight: bfloat16 [2304, 16], P('fsdp'), may hold values from -0.125 to 0.125
Outputs:
- query_grad: bfloat16 [8, 4096, 2048], P('fsdp', 'ctx')
- key_grad: bfloat16 [8, 4096, 2048], P('fsdp', 'ctx')
- value_grad: bfloat16 [8, 4096, 2048], P('fsdp', 'ctx')
- hidden_grad: bfloat16 [8, 4096, 2304], P('fsdp', 'ctx')
- gate_down_grad: float32 [2304, 128], P('fsdp')
- gate_up_grad: float32 [128, 2048], P(None, 'fsdp')
- beta_weight_grad: float32 [2304, 16], P('fsdp')
- gate_bias_grad: float32 [2048], replicated
- decay_rate_grad: float32 [2048], replicated
All inputs are finite; a program needn't handle non-finite values.
Results may differ from a plain program's by a relative error of at most 0.0052.
Values may be sent and summed in bfloat16 or wider, within the bound.
No kernel may reach another device: no remote copies, remote signals or barrier semaphores. Data moves between devices by JAX's collectives and lax.ppermute only.
A program may use at most 256 MiB of HBM per device.

v0:
```python
import jax
import jax.numpy as jnp
from jax import lax
from jax.sharding import PartitionSpec as P

CH = 128


PRECISE = lax.Precision.HIGHEST
EPSILON = 1e-06


def carried_in(value, axis, join, neutral):
    count, mine = (lax.axis_size(axis), lax.axis_index(axis))
    pieces = jax.tree.map(lambda part: lax.all_gather(part, axis), value)
    pieces = jax.tree.map(lambda part: part[::-1], pieces)
    mine = count - 1 - mine
    so_far = jax.tree.map(
        lambda part, zero: jnp.full_like(part, 0) + jnp.asarray(zero, part.dtype), value, neutral
    )

    def turn(position, so_far):
        longer = join(so_far, jax.tree.map(lambda part: part[position], pieces))
        return jax.tree.map(lambda new, old: jnp.where(position < mine, new, old), longer, so_far)

    return lax.fori_loop(0, count - 1, turn, so_far)


def unit_rows(matrix):
    return matrix * lax.rsqrt(jnp.sum(matrix * matrix, axis=-1, keepdims=True) + EPSILON)


def to_spans(values):
    tok_rows = values.shape[0]
    return values.reshape((tok_rows // CH, CH) + values.shape[1:]).swapaxes(1, 2)


def tri_masks():
    row_index = lax.broadcasted_iota(jnp.int32, (CH, CH), 0)
    col_index = lax.broadcasted_iota(jnp.int32, (CH, CH), 1)
    return (
        (row_index > col_index).astype(jnp.float32),
        (row_index >= col_index).astype(jnp.float32),
    )


def span_terms(k_span, g_span, b_span):
    cumulative = jnp.cumsum(g_span, axis=1)
    key_plus = k_span * jnp.exp(cumulative)
    key_minus = k_span * jnp.exp(-cumulative)
    key_end = k_span * jnp.exp(cumulative[:, -1:, :] - cumulative)
    strict, _ = tri_masks()
    mixing = (
        jnp.einsum("htc,hsc->hts", key_plus, key_minus, precision=PRECISE)
        * strict
        * b_span[:, :, None]
    )
    system = mixing + jnp.eye(CH, dtype=jnp.float32)
    return (cumulative, key_plus, key_minus, key_end, system)


def block_forward(start_state, queries, keys_in, values_in, decay_heads, beta_gate):
    q_all = to_spans(unit_rows(queries))
    k_all = to_spans(unit_rows(keys_in))
    v_all = to_spans(values_in)
    g_all = to_spans(decay_heads)
    b_all = to_spans(beta_gate)
    _, inclusive = tri_masks()

    def block_advance(carried, pieces):
        q_span, k_span, v_span, g_span, b_span = pieces
        cumulative, key_plus, key_minus, key_end, system = span_terms(k_span, g_span, b_span)
        query_plus = q_span * jnp.exp(cumulative)
        target = b_span[:, :, None] * (
            v_span - jnp.einsum("htc,hcd->htd", key_plus, carried, precision=PRECISE)
        )
        updates = jax.scipy.linalg.solve_triangular(system, target, lower=True, unit_diagonal=True)
        scores = jnp.einsum("htc,hsc->hts", query_plus, key_minus, precision=PRECISE) * inclusive
        outputs = jnp.einsum("htc,hcd->htd", query_plus, carried, precision=PRECISE) + jnp.einsum(
            "hts,hsd->htd", scores, updates, precision=PRECISE
        )
        renewed = jnp.exp(cumulative[:, -1, :])[:, :, None] * carried + jnp.einsum(
            "hsc,hsd->hcd", key_end, updates, precision=PRECISE
        )
        return (renewed, outputs)

    end_state, outputs = lax.scan(block_advance, start_state, (q_all, k_all, v_all, g_all, b_all))
    return (outputs.swapaxes(1, 2).reshape(queries.shape), end_state)


def transition(keys_in, decay_heads, beta_gate, identity):
    k_all = to_spans(unit_rows(keys_in))
    g_all = to_spans(decay_heads)
    b_all = to_spans(beta_gate)

    def transition_advance(product, pieces):
        k_span, g_span, b_span = pieces
        cumulative, key_plus, key_minus, key_end, system = span_terms(k_span, g_span, b_span)
        solved = jax.scipy.linalg.solve_triangular(
            system, b_span[:, :, None] * key_plus, lower=True, unit_diagonal=True
        )
        moving = jnp.exp(cumulative[:, -1, :])[:, :, None] * identity - jnp.einsum(
            "hsc,hse->hce", key_end, solved, precision=PRECISE
        )
        return (jnp.einsum("hce,hef->hcf", moving, product, precision=PRECISE), None)

    result, _ = lax.scan(transition_advance, identity, (k_all, g_all, b_all))
    return result


def combine(earlier, later):
    first_map, first_sum = earlier
    second_map, second_sum = later
    joined_map = jnp.einsum("hab,hbc->hac", first_map, second_map, precision=PRECISE)
    joined_sum = jnp.einsum("hba,hbc->hac", second_map, first_sum, precision=PRECISE) + second_sum
    return (joined_map, joined_sum)


def gate_forward(hidden_rows, down_full, up_full, gate_bias, decay_rate, beta_full):
    low_rank = jnp.dot(hidden_rows, down_full, preferred_element_type=jnp.float32).astype(
        jnp.bfloat16
    )
    gate_input = jnp.dot(low_rank, up_full, preferred_element_type=jnp.float32) + gate_bias
    log_decay = -decay_rate * jax.nn.softplus(gate_input)
    beta_gate = jax.nn.sigmoid(jnp.dot(hidden_rows, beta_full, preferred_element_type=jnp.float32))
    return (low_rank, gate_input, log_decay, beta_gate)


def contract_rows(left, right):
    return lax.dot_general(
        left, right, (((0,), (0,)), ((), ())), preferred_element_type=jnp.float32
    )


def contract_cols(left, right):
    return lax.dot_general(
        left, right, (((1,), (1,)), ((), ())), preferred_element_type=jnp.float32
    )


def gate_backward(
    hidden_rows,
    low_rank,
    gate_input,
    beta_gate,
    decay_cot,
    beta_cot,
    down_full,
    up_full,
    decay_rate,
    beta_full,
):
    input_grad = decay_cot * -decay_rate * jax.nn.sigmoid(gate_input)
    input_half = input_grad.astype(jnp.bfloat16)
    rate_term = -jnp.sum(decay_cot * jax.nn.softplus(gate_input), axis=0)
    bias_term = jnp.sum(input_grad, axis=0)
    up_term = contract_rows(low_rank, input_half)
    low_grad = contract_cols(input_half, up_full).astype(jnp.bfloat16)
    score_grad = (beta_cot * beta_gate * (1.0 - beta_gate)).astype(jnp.bfloat16)
    down_term = contract_rows(hidden_rows, low_grad)
    beta_term = contract_rows(hidden_rows, score_grad)
    hidden_grad = (
        contract_cols(low_grad, down_full) + contract_cols(score_grad, beta_full)
    ).astype(jnp.bfloat16)
    return (hidden_grad, down_term, up_term, beta_term, bias_term, rate_term)


def on_device(
    hidden,
    query_heads,
    key_heads,
    value_heads,
    out_grad,
    checkpoint,
    gate_down,
    gate_up,
    gate_bias,
    decay_rate,
    beta_weight,
):
    tok_rows, model_width = (hidden.shape[1], hidden.shape[2])
    count_heads, size_head = (checkpoint.shape[2], checkpoint.shape[3])
    down_full, beta_full, up_full = (
        lax.all_gather(gate_down, "fsdp", axis=0, tiled=True),
        lax.all_gather(beta_weight, "fsdp", axis=0, tiled=True),
        lax.all_gather(gate_up, "fsdp", axis=1, tiled=True),
    )
    hidden_rows = hidden.reshape(tok_rows, model_width)
    low_rank, gate_input, log_decay, beta_gate = gate_forward(
        hidden_rows, down_full, up_full, gate_bias, decay_rate, beta_full
    )

    def per_head(values):
        return values.reshape(tok_rows, count_heads, size_head).astype(jnp.float32)

    start_state = checkpoint.reshape(count_heads, size_head, size_head)
    keys_in = per_head(key_heads)
    decay_heads = log_decay.reshape(tok_rows, count_heads, size_head)
    _, pullback = jax.vjp(
        block_forward,
        start_state,
        per_head(query_heads),
        keys_in,
        per_head(value_heads),
        decay_heads,
        beta_gate,
    )
    cotangent = per_head(out_grad)
    local_sum = pullback((cotangent, jnp.zeros_like(start_state)))[0]
    identity = jnp.broadcast_to(jnp.eye(size_head, dtype=jnp.float32), start_state.shape)
    moving = transition(keys_in, decay_heads, beta_gate, identity)
    _, end_grad = carried_in(
        (moving, local_sum), "ctx", combine, (identity, jnp.zeros_like(start_state))
    )
    start_grad, q_grad, k_grad, v_grad, decay_cot, beta_cot = pullback((cotangent, end_grad))
    hidden_grad, down_term, up_term, beta_term, bias_term, rate_term = gate_backward(
        hidden_rows,
        low_rank,
        gate_input,
        beta_gate,
        decay_cot.reshape(tok_rows, -1),
        beta_cot,
        down_full,
        up_full,
        decay_rate,
        beta_full,
    )
    summed = lax.psum((down_term, beta_term, up_term, bias_term, rate_term), "ctx")
    shards = (
        lax.psum_scatter(summed[0], "fsdp", scatter_dimension=0, tiled=True),
        lax.psum_scatter(summed[1], "fsdp", scatter_dimension=0, tiled=True),
        lax.psum_scatter(summed[2], "fsdp", scatter_dimension=1, tiled=True),
    )
    vectors = lax.psum((summed[3], summed[4]), "fsdp")

    def restore(values):
        return values.reshape(1, tok_rows, -1).astype(jnp.bfloat16)

    return (
        restore(q_grad),
        restore(k_grad),
        restore(v_grad),
        hidden_grad.reshape(1, tok_rows, model_width),
        shards[0],
        shards[2],
        shards[1],
        vectors[0],
        vectors[1],
    )


def solution(mesh):
    return jax.shard_map(
        on_device,
        mesh=mesh,
        in_specs=(
            P("fsdp", "ctx", None),
            P("fsdp", "ctx", None),
            P("fsdp", "ctx", None),
            P("fsdp", "ctx", None),
            P("fsdp", "ctx", None),
            P("fsdp", "ctx", None, None, None),
            P("fsdp", None),
            P(None, "fsdp"),
            P(),
            P(),
            P("fsdp", None),
        ),
        out_specs=(
            P("fsdp", "ctx", None),
            P("fsdp", "ctx", None),
            P("fsdp", "ctx", None),
            P("fsdp", "ctx", None),
            P("fsdp", None),
            P(None, "fsdp"),
            P("fsdp", None),
            P(),
            P(),
        ),
        check_vma=False,
    )
```

profile of v0, /device:TPU:32, one launch (start us, length us, event | category | flops | bytes accessed | tf_op | source)
XLA Modules:
  0.0 1254.7 jit_solution(2753471399304842090)
XLA Ops:
  12.4 13.6 %all_gather.21 = bf16[2304,128]{1,0:T(8,128)(2,1)S(1)} all-gather(bf16[288,128]{1,0:T(8,128)(2,1)S(1)} %copy-done.46), channel_id=1, replica_groups=mesh['fsdp'=8,'ctx'=32] {'fsdp'}, dimensions={0}, use_global_device_ids=true | all-gather | bytes 663552 | tf_op jit(solution)/shard_map/all_gather | solution.py:184
  26.1 13.1 %all_gather.22 = bf16[128,2048]{1,0:T(8,128)(2,1)S(1)} all-gather(bf16[128,256]{1,0:T(8,128)(2,1)S(1)} %copy-done.47), channel_id=1, replica_groups=mesh['fsdp'=8,'ctx'=32] {'fsdp'}, dimensions={1}, use_global_device_ids=true | all-gather | bytes 589824 | tf_op jit(solution)/shard_map/all_gather | solution.py:186
  41.3 23.2 %fusion.20 = f32[16,128,128]{2,0,1:T(8,128)S(1)} fusion(f32[1,128,16,128]{3,2,1,0:T(8,128)S(1)} %bitcast.382), kind=kOutput, calls=%fused_computation.48 | output fusion | flops 33292288 | bytes 2097152 | tf_op jit(solution)/shard_map/jvp()/while/body/eval_jaxpr/jit(cumsum)/reduce_window_sum | solution.py:48
  66.1 2.5 copy.144
  69.9 2.9 convolution_multiply_fusion.1
  76.8 4.1 convolution_multiply_fusion.2
  80.9 13.2 %all-gather.2 = bf16[8,288,16]{1,2,0:T(8,128)(2,1)S(1)} all-gather(bf16[1,288,16]{1,2,0:T(8,128)(2,1)S(1)} %bitcast.402), channel_id=1, replica_groups=mesh['fsdp'=8,'ctx'=32] {'fsdp'}, dimensions={0}, use_global_device_ids=true | all-gather | bytes 82944 | tf_op jit(solution)/shard_map/all_gather | solution.py:185
  96.8 2.5 add_bitcast_fusion
  99.3 158.6 %custom-call.10 = f32[16,1,128,128]{2,3,1,0:T(8,128)} custom-call(f32[16,1,128,128]{3,2,1,0:T(8,128)} %add_bitcast_fusion), custom_call_target="InvertDiagBlocksLowerTriangular" | custom-call | tf_op jit(solution)/shard_map/jvp()/while/body/eval_jaxpr/jit(_solve_triangular)/vmap()/triangular_solve/custom-call.1 | solution.py:77
  258.0 3.2 convolution_add_fusion.8
  262.4 3.4 convolution_add_fusion.6
  265.9 3.8 fusion.47
  269.7 2.6 convolution_subtract_fusion
  274.6 2.6 copy.137
  277.1 2.5 copy.166
  284.1 2.6 fusion.58
  295.2 3.3 convolution_add_fusion.9
  298.5 200.7 %all-gather.8.cloned.1.call-done = f32[512,128,128]{2,1,0:T(8,128)} async-done(((f32[16,128,128]{2,1,0:T(8,128)}), f32[512,128,128]{2,1,0:T(8,128)}) %all-gather.8.cloned.1.call-update) | async-done | bytes 33554448 | tf_op jit(solution)/shard_map/all_gather | solution.py:15
  499.2 23.4 %rev.7 = f32[32,16,128,128]{3,2,1,0:T(8,128)} reverse(f32[32,16,128,128]{3,2,1,0:T(8,128)} %bitcast.372), dimensions={0} | reverse | bytes 67108864 | tf_op jit(solution)/shard_map/rev | solution.py:16
  522.6 209.2 %all-gather.6.cloned.1.call-done = f32[512,128,128]{2,1,0:T(8,128)} async-done(((f32[16,128,128]{2,1,0:T(8,128)}), f32[512,128,128]{2,1,0:T(8,128)}) %all-gather.6.cloned.1.call-update) | async-done | bytes 33554448 | tf_op jit(solution)/shard_map/all_gather | solution.py:15
  731.8 33.4 %copy.143 = f32[32,16,128,128]{2,3,1,0:T(8,128)} copy(f32[32,16,128,128]{3,2,1,0:T(8,128)} %bitcast.373) | data formatting | bytes 67108864 | tf_op jit(solution)/shard_map/all_gather | solution.py:15
  765.2 23.0 %rev.6 = f32[32,16,128,128]{2,3,1,0:T(8,128)} reverse(f32[32,16,128,128]{2,3,1,0:T(8,128)} %copy.143), dimensions={0} | reverse | bytes 67108864 | tf_op jit(solution)/shard_map/rev | solution.py:16
  788.2 155.8 %while.10 = (s32[]{:T(128)}, f32[16,128,128]{2,1,0:T(8,128)}, s32[]{:T(128)}, f32[32,16,128,128]{2,3,1,0:T(8,128)}, f32[32,16,128,128]{3,2,1,0:T(8,128)}, /*index=5*/s32[]{:T(128)}, s32[]{:T(128)}) while((s32[]{:T(128)}, f32[16,128,128]{2,1,0:T(8,128)}, s32[]{:T(128)}, f32[32,16,128,128]{2,3,1,0:T(8,128)}, ...), condition=%wide.region_5.8_spmd.clone, body=%wide.region_4.7_spmd.clone.sunk | while | flops 403701760 | bytes 7342687 | solution.py:26
  789.4 3.8 fusion.166
  794.4 3.8 fusion.166
  799.5 3.8 fusion.166
  804.5 3.8 fusion.166
  809.5 3.8 fusion.166
  814.5 3.8 fusion.166
  819.5 3.8 fusion.166
  824.5 3.8 fusion.166
  829.5 3.8 fusion.166
  834.6 3.8 fusion.166
  839.6 3.8 fusion.166
  844.6 3.8 fusion.166
  849.6 3.8 fusion.166
  854.6 3.8 fusion.166
  859.6 3.8 fusion.166
  864.6 3.8 fusion.166
  869.6 3.8 fusion.166
  874.7 3.8 fusion.166
  879.7 3.8 fusion.166
  884.7 3.8 fusion.166
  889.7 3.8 fusion.166
  894.7 3.8 fusion.166
  899.7 3.8 fusion.166
  904.7 3.8 fusion.166
  909.8 3.8 fusion.166
  914.8 3.8 fusion.166
  919.8 3.8 fusion.166
  924.8 3.8 fusion.166
  929.8 3.8 fusion.166
  934.8 3.8 fusion.166
  939.8 3.8 fusion.166
  944.0 3.2 convolution_add_fusion.5
  950.8 2.6 fusion.68
  960.3 2.7 convolution_add_fusion.4
  963.0 3.8 fusion.21
  969.1 2.6 fusion.61
  980.2 28.6 %reduce-scatter.10.cloned.1.call-done = f32[288,128]{1,0:T(8,128)} async-done(((f32[2304,128]{1,0:T(8,128)}), f32[288,128]{1,0:T(8,128)}) %reduce-scatter.10.cloned.1.call-update) | async-done | bytes 147472
  1010.5 34.3 %reduce-scatter.8.cloned.1.call-done = f32[128,256]{1,0:T(8,128)} async-done(((f32[128,2048]{1,0:T(8,128)}), f32[128,256]{1,0:T(8,128)}) %reduce-scatter.8.cloned.1.call-update) | async-done | bytes 131088 | tf_op jit(solution)/shard_map/reduce_scatter | solution.py:232
  1056.9 24.2 %reduce-scatter.12.cloned.1.call-done = f32[288,16]{1,0:T(8,128)} async-done(((f32[2304,16]{1,0:T(8,128)}), f32[288,16]{1,0:T(8,128)}) %reduce-scatter.12.cloned.1.call-update) | async-done | bytes 18448
  1082.1 138.2 %all-reduce.2 = (f32[288,16]{0,1:T(8,128)}, f32[2048]{0:T(1024)S(1)}, f32[2048]{0:T(1024)S(1)}) all-reduce(f32[288,16]{0,1:T(8,128)S(1)} %copy.206, f32[2048]{0:T(1024)S(1)} %get-tuple-element.434, f32[2048]{0:T(1024)S(1)} %neg.70), channel_id=1, replica_groups=mesh['fsdp'=8,'ctx'=32] {'ctx'}, use_global_device_ids=true, to_apply=%region_16.19 | all-reduce | flops 8704 | bytes 69632 | tf_op jit(solution)/shard_map/psum | solution.py:228
  1220.3 24.2 %all-reduce.4 = (f32[2048]{0:T(1024)}, f32[2048]{0:T(1024)}) all-reduce(f32[2048]{0:T(1024)S(1)} %get-tuple-element.428, f32[2048]{0:T(1024)S(1)} %get-tuple-element.429), channel_id=1, replica_groups=mesh['fsdp'=8,'ctx'=32] {'fsdp'}, use_global_device_ids=true, to_apply=%region_20.23 | all-reduce | flops 4096 | bytes 32768 | tf_op jit(solution)/shard_map/psum | solution.py:234
  (214 shorter events, 110.0 us)
Async XLA Ops:
  7.2 32.0 %copy-start = (bf16[1,128,2304]{2,1,0:T(8,128)(2,1)S(1)}, bf16[1,128,2304]{2,1,0:T(8,128)(2,1)}, u32[]{:S(2)}) copy-start(bf16[1,128,2304]{2,1,0:T(8,128)(2,1)} %param.17) | copy-start | bytes 1769476
  7.2 492.0 %all-gather.8.cloned.1.call-start = ((), (), s32[]{:S(2)}) async-start(), calls=%async_computation.4 | async-start | bytes 34603008 | tf_op jit(solution)/shard_map/all_gather | solution.py:15
  9.7 1.2 copy-start.28
  9.8 1.4 copy-start.39
  9.8 1.0 copy-start.12
  11.2 58.5 %copy-start.44 = (f32[128,16]{0,1:T(8,128)}, f32[128,16]{0,1:T(8,128)S(1)}, u32[]{:S(2)}) copy-start(f32[128,16]{0,1:T(8,128)S(1)} %multiply_reduce_fusion.2) | copy-start | bytes 24580
  11.5 0.8 copy-start.30
  11.5 1.0 copy-start.46
  11.6 27.9 %copy-start.13 = (f32[1,128,2048]{1,2,0:T(8,128)}, f32[1,128,2048]{1,2,0:T(8,128)S(1)}, u32[]{:S(2)}) copy-start(f32[1,128,2048]{1,2,0:T(8,128)S(1)} %convert_element_type.168) | copy-start | bytes 3145732
  11.6 14.5 %copy-start.47 = (bf16[128,256]{1,0:T(8,128)(2,1)S(1)}, bf16[128,256]{1,0:T(8,128)(2,1)}, u32[]{:S(2)}) copy-start(bf16[128,256]{1,0:T(8,128)(2,1)} %param.24) | copy-start | bytes 196612
  11.6 27.6 %copy-start.50 = (f32[2048]{0:T(1024)S(1)}, f32[2048]{0:T(1024)}, u32[]{:S(2)}) copy-start(f32[2048]{0:T(1024)} %param.26) | copy-start | bytes 24580
  12.4 27.5 %copy-start.49 = (f32[2048]{0:T(1024)S(1)}, f32[2048]{0:T(1024)}, u32[]{:S(2)}) copy-start(f32[2048]{0:T(1024)} %param.25) | copy-start | bytes 24580
  26.1 13.1 %copy-start.24 = (bf16[2304,128]{1,0:T(8,128)(2,1)}, bf16[2304,128]{1,0:T(8,128)(2,1)S(1)}, u32[]{:S(2)}) copy-start(bf16[2304,128]{1,0:T(8,128)(2,1)S(1)} %all_gather.21) | copy-start | bytes 1769476
  39.2 0.8 copy-start.26
  40.0 0.9 copy-start.40
  40.3 1.0 copy-start.18
  68.6 1.3 copy-start.5
  68.9 1.0 copy-start.38
  69.6 897.2 %copy-start.42 = (f32[128,16]{0,1:T(8,128)}, f32[128,16]{0,1:T(8,128)S(1)}, u32[]{:S(2)}) copy-start(f32[128,16]{0,1:T(8,128)S(1)} %get-tuple-element.453) | copy-start | bytes 24580
  69.9 2.9 copy-start.23
  73.5 1.0 copy-start.20
  76.8 4.1 copy-start.48
  258.0 3.2 copy-start.2
  258.0 3.2 copy-start.36
  265.8 465.9 %all-gather.6.cloned.1.call-start = ((), (), s32[]{:S(2)}) async-start(), calls=%async_computation.3 | async-start | bytes 34603008 | tf_op jit(solution)/shard_map/all_gather | solution.py:15
  274.3 734.5 %reduce-scatter.10.cloned.1.call-start = ((), (), s32[]{:S(2)}) async-start(), calls=%async_computation.6 | async-start | bytes 1327104
  284.0 2.6 copy-start.8
  284.0 2.6 copy-start.35
  286.7 1.6 copy-start.3
  288.2 2.2 copy-start.14
  290.4 1.0 copy-start.10
  291.4 1.3 copy-start.6
  944.0 3.2 copy-start.4
  947.2 1.2 copy-start.11
  948.4 8.6 copy-start.16
  948.4 2.3 copy-start.1
  950.8 2.6 copy-start.9
  953.4 1.2 copy-start.22
  957.1 3.2 copy-start.37
  960.2 2.8 copy-start.21
  960.2 2.8 copy-start.33
  960.2 2.8 copy-start.34
  963.0 3.8 copy-start.7
  969.1 2.6 copy-start.19
  971.7 1.0 copy-start.27
  974.9 0.8 copy-start.41
  974.9 2.1 copy-start.15
  974.9 2.1 copy-start.17
  974.9 69.9 %reduce-scatter.8.cloned.1.call-start = ((), (), s32[]{:S(2)}) async-start(), calls=%async_computation.5 | async-start | bytes 1179648 | tf_op jit(solution)/shard_map/reduce_scatter | solution.py:232
  976.9 104.2 %reduce-scatter.12.cloned.1.call-start = ((), (), s32[]{:S(2)}) async-start(), calls=%async_computation.7 | async-start | bytes 1327104
  978.3 1.5 copy-start.25
  979.8 264.7 %all-reduce.7.cloned.1.call-start = ((), (), s32[]{:S(2)}) async-start(), calls=%async_computation.8 | async-start | bytes 655360 | tf_op jit(solution)/shard_map/psum | solution.py:228
  979.8 65.0 %copy-start.45 = (f32[128,16]{0,1:T(8,128)S(1)}, f32[128,16]{0,1:T(8,128)}, u32[]{:S(2)}) copy-start(f32[128,16]{0,1:T(8,128)} %copy-done.44) | copy-start | bytes 24580
  1044.8 2.5 copy-start.32
  1047.3 1.3 copy-start.31
  1051.0 1.6 copy-start.29
  1051.0 1.6 copy-start.43
Sparse Core Ops, SparseCore 0:
  266.0 233.1 all-gather.7
  501.7 230.0 all-gather.5
  975.0 33.7 reduce-scatter.9
  1011.2 33.5 reduce-scatter.7
  1047.2 33.8 reduce-scatter.11
  1084.5 144.7 all-reduce.6
where the time goes:
time: 1270 us; the launch traced here: 1250 us
  waiting for transfers between devices  497 us (39%)
  blocking collectives  202 us (16%)
  other arithmetic  199 us (16%)
  matrix products  182 us (14%)
  local copies, waits for them, and re-layouts  159 us (13%)
  between operations  15.1 us (1%)
    all_gather x2, waiting for transfers between devices, carried_in(): pieces = jax.tree.map(lambda part: lax.all_gather(part, axis), value)  410 us
    another operation x5, other arithmetic, block_advance(): jax.scipy.linalg.solve_triangular(system, target, lower=True, unit_diagon...  163 us
    psum x1, blocking collectives, on_device(): lax.psum((down_term, beta_term, up_term, bias_term, rate_term), 'ctx')  138 us
    dot_general x31, matrix products, combine(): jnp.einsum('hba,hbc->hac', second_map, first_sum, precision=PRECISE)  117 us
    unnamed x8, waiting for transfers between devices  53 us
    rev x2, local copies, waits for them, and re-layouts, carried_in(): pieces = jax.tree.map(lambda part: part[::-1], pieces)  46.4 us
    while x31, local copies, waits for them, and re-layouts  38 us
    reduce_scatter x1, waiting for transfers between devices, on_device(): lax.psum_scatter(summed[2], 'fsdp', scatter_dimension=1, tiled=True)  34.3 us
  transfers between devices with their start and end apart: 6, of which 5 were waited for; matrix products, arithmetic and copies ran while one was open for 6% of the time, Pallas kernels for 0%

commit v1 on v0

v1 whole, which is shorter than its diff:
```python
import functools

import jax
import jax.numpy as jnp
from jax import lax
from jax.experimental import pallas as pl
from jax.experimental.pallas import tpu as pltpu
from jax.sharding import Mesh, PartitionSpec as P

EPSILON = 1e-06
BF = jnp.bfloat16
F32 = jnp.float32
N = 128
HB = 4
FIRST_HB = 8
INTERPRET = False


def split(x):
    hi = x.astype(BF)
    return [hi, (x - hi.astype(F32)).astype(BF)]


def split3(x):
    hi = x.astype(BF)
    rest = x - hi.astype(F32)
    mid = rest.astype(BF)
    return [hi, mid, (rest - mid.astype(F32)).astype(BF)]


def dot(a, b, ca=1, cb=0):
    return lax.dot_general(a, b, (((ca,), (cb,)), ((), ())), preferred_element_type=F32)


def mm(a, b, ca=1, cb=0):
    if len(a) > 1 and len(b) > 1:
        both = jnp.concatenate(b, axis=1 - cb)
        both = dot(jnp.concatenate(a, axis=ca), jnp.concatenate([both, both], axis=cb), ca, cb)
        half = both.shape[1] // 2
        return both[:, :half] + both[:, half:]
    if len(a) > 1:
        return dot(jnp.concatenate(a, axis=ca), jnp.concatenate([b[0], b[0]], axis=cb), ca, cb)
    return sum(dot(a[0], part, ca, cb) for part in b)


def iotas():
    return lax.broadcasted_iota(jnp.int32, (N, N), 0), lax.broadcasted_iota(jnp.int32, (N, N), 1)


def ones_where(cond):
    return jnp.where(cond, 1.0, 0.0).astype(BF)


def softplus(x):
    return jnp.maximum(x, 0.0) + jnp.log1p(jnp.exp(-jnp.abs(x)))


def unit(x):
    scale = lax.rsqrt(jnp.sum(x * x, axis=-1, keepdims=True) + EPSILON)
    return x * scale, scale


def column(values, index):
    lane = lax.broadcasted_iota(jnp.int32, values.shape, 1)
    return jnp.sum(jnp.where(lane == index, values, 0.0), axis=1, keepdims=True)


def inverses(stricts, row, col):
    near = (row >> 3) == (col >> 3)
    gather = ones_where(near)
    lane = lax.broadcasted_iota(jnp.int32, (8, N), 1) & 7
    sub = lax.broadcasted_iota(jnp.int32, (8, N), 0)
    invs = []
    for strict in stricts:
        block = jnp.where(near, strict, 0.0)
        block = sum(block[8 * i:8 * i + 8] for i in range(N // 8))
        picked = split3(jnp.concatenate([jnp.where(lane == k, block, 0.0) for k in range(8)], axis=0))
        spread = sum(dot(part, gather) for part in picked)
        inv = jnp.where(lane == sub, 1.0, 0.0)
        for k in range(7):
            inv = inv - spread[8 * k:8 * k + 8] * inv[k:k + 1, :]
        invs.append(jnp.where(near, jnp.concatenate([inv] * (N // 8), axis=0), 0.0))
    for bit in range(3, 7):
        pick = ((row >> (bit + 1)) == (col >> (bit + 1))) & ((row >> bit) != (col >> bit))
        parts = [split(inv) for inv in invs]
        offs = [split(jnp.where(pick, strict, 0.0)) for strict in stricts]
        offs = [split(mm(part, off)) for part, off in zip(parts, offs)]
        invs = [inv - mm(off, part) for inv, off, part in zip(invs, offs, parts)]
    return invs


def head_columns(count):
    return [slice(i * N, (i + 1) * N) for i in range(count)]


def first_kernel(low_ref, up_ref, bias_ref, rate_ref, beta_ref, q_ref, k_ref, g_ref,
                 send_ref, inv_ref, mix_ref, sco_ref, cum_ref):
    count = inv_ref.shape[0]
    base = pl.program_id(0) * count
    row, col = iotas()
    tri = ones_where(row >= col)
    cols = head_columns(count)
    each = lambda f: [f(i) for i in range(count)]
    gate = each(lambda i: dot(low_ref[...], up_ref[i]) + bias_ref[:, cols[i]])
    decay = each(lambda i: split3(-rate_ref[:, cols[i]] * softplus(gate[i])))
    cum = each(lambda i: sum(dot(tri, piece) for piece in decay[i]))
    for i in range(count):
        cum_ref[i] = cum[i]
    last = each(lambda i: cum[i][N - 1:N, :])
    qn = each(lambda i: unit(q_ref[:, cols[i]].astype(F32))[0])
    kn = each(lambda i: unit(k_ref[:, cols[i]].astype(F32))[0])
    scale = each(lambda i: jnp.exp(cum[i]))
    kp = each(lambda i: kn[i] * scale[i])
    qp = each(lambda i: qn[i] * scale[i])
    km = each(lambda i: split(kn[i] * jnp.exp(-cum[i])))
    beta = each(lambda i: column(beta_ref[...], base + i))
    mix = each(lambda i: jnp.where(row > col, mm(split(kp[i]), km[i], 1, 1), 0.0))
    sco = each(lambda i: jnp.where(row >= col, mm(split(qp[i]), km[i], 1, 1), 0.0))
    for i in range(count):
        mix_ref[i] = mix[i]
        sco_ref[i] = sco[i]
    inv = inverses(each(lambda i: mix[i] * beta[i]), row, col)
    for i in range(count):
        inv_ref[i] = inv[i]
    z = each(lambda i: split(mm(split(inv[i]), split(kp[i] * beta[i]))))
    seen = each(lambda i: split(qp[i] - mm(split(sco[i]), z[i])))
    local = each(lambda i: mm(seen[i], [g_ref[:, cols[i]]], 0, 0))
    ke = each(lambda i: split(kn[i] * jnp.exp(last[i] - cum[i])))
    moving = each(lambda i: jnp.where(row == col, jnp.exp(last[i]), 0.0) - mm(z[i], ke[i], 0, 0))
    for i in range(count):
        send_ref[i, 0:N, :] = moving[i].astype(BF)
        send_ref[i, N:2 * N, :] = local[i].astype(BF)


def chain_kernel(got_ref, all_ref, tot_ref):
    blocks, heads = got_ref.shape[0], got_ref.shape[1]
    each = lambda f: [f(h) for h in range(heads)]
    both = each(lambda h: jnp.concatenate(
        [got_ref[blocks - 1, h, 0:N, :], got_ref[blocks - 1, h, N:2 * N, :]], axis=1).astype(F32))
    for j in range(blocks - 1, -1, -1):
        if j < blocks - 1:
            both = each(lambda h: mm([got_ref[j, h, 0:N, :]], split(both[h])))
            both = each(lambda h: jnp.concatenate(
                [both[h][:, :N], both[h][:, N:] + got_ref[j, h, N:2 * N, :].astype(F32)], axis=1))
        for h in range(heads):
            all_ref[j, h] = both[h]
    for h in range(heads):
        tot_ref[h] = both[h].astype(BF)


def apply_kernel(all_ref, *refs):
    *later, end_ref = refs
    blocks, heads = all_ref.shape[0], all_ref.shape[1]
    each = lambda f: [f(h) for h in range(heads)]
    carry = each(lambda h: jnp.zeros((N, N), F32))
    for ref in later:
        carry = each(lambda h: mm([ref[h, :, 0:N]], split(carry[h])) + ref[h, :, N:2 * N].astype(F32))
    for h in range(heads):
        end_ref[blocks - 1, h] = carry[h].astype(BF)
    carry = each(lambda h: split(carry[h]))
    for j in range(blocks - 1):
        for h in range(heads):
            end_ref[j, h] = (mm(split(all_ref[j + 1, h, :, :N]), carry[h])
                             + all_ref[j + 1, h, :, N:]).astype(BF)


def middle_kernel(beta_ref, q_ref, k_ref, v_ref, g_ref, start_ref, inv_ref, sco_ref, cum_ref,
                  qg_ref, rest_ref, upd_ref, y_ref, kms_ref, term_ref):
    count = inv_ref.shape[0]
    base = pl.program_id(0) * count
    row, col = iotas()
    cols = head_columns(count)
    each = lambda f: [f(i) for i in range(count)]
    cum = each(lambda i: cum_ref[i])
    q = each(lambda i: unit(q_ref[:, cols[i]].astype(F32)))
    kn = each(lambda i: unit(k_ref[:, cols[i]].astype(F32))[0])
    plus = each(lambda i: jnp.exp(cum[i]))
    qp = each(lambda i: q[i][0] * plus[i])
    km = each(lambda i: split(kn[i] * jnp.exp(-cum[i])))
    beta = each(lambda i: column(beta_ref[...], base + i))
    grad = each(lambda i: [g_ref[:, cols[i]]])
    start = each(lambda i: split(start_ref[i]))
    inv = each(lambda i: split(inv_ref[i]))
    rest = each(lambda i: v_ref[:, cols[i]].astype(F32) - mm(split(kn[i] * plus[i]), start[i]))
    upd = each(lambda i: mm(inv[i], split(rest[i] * beta[i])))
    y = each(lambda i: mm(inv[i], split(mm(split(sco_ref[i]), grad[i], 0, 0)), 0, 0))
    upd_s = each(lambda i: split(upd[i]))
    sco_cot = each(lambda i: split(jnp.where(row >= col, mm(grad[i], upd_s[i], 1, 1), 0.0)))
    qp_cot = each(lambda i: mm(grad[i], start[i], 1, 1) + mm(sco_cot[i], km[i]))
    kms = each(lambda i: mm(sco_cot[i], split(qp[i]), 0, 0))
    qn_cot = each(lambda i: qp_cot[i] * plus[i])
    for i in range(count):
        rest_ref[i] = rest[i]
        upd_ref[i] = upd[i]
        y_ref[i] = y[i]
        kms_ref[i] = kms[i]
        term_ref[i] = qp_cot[i] * qp[i]
        qg_ref[:, i * N:(i + 1) * N] = (q[i][1] * (
            qn_cot[i] - q[i][0] * jnp.sum(qn_cot[i] * q[i][0], axis=1, keepdims=True))).astype(BF)


def second_kernel(low_ref, up_ref, bias_ref, rate_ref, beta_ref, k_ref, start_ref, end_ref,
                  inv_ref, mix_ref, cum_ref, rest_ref, upd_ref, y_ref, kms_ref, term_ref,
                  kg_ref, vg_ref, half_ref, vec_ref, lowg_ref, score_ref, low_acc, score_acc):
    count = inv_ref.shape[0]
    step = pl.program_id(0)
    base = step * count
    row, col = iotas()
    upper = ones_where(row <= col)
    ones = jnp.ones((8, N), BF)

    @pl.when(step == 0)
    def _():
        low_acc[...] = jnp.zeros_like(low_acc)
        score_acc[...] = jnp.zeros_like(score_acc)

    cols = head_columns(count)
    each = lambda f: [f(i) for i in range(count)]
    cum = each(lambda i: cum_ref[i])
    last = each(lambda i: cum[i][N - 1:N, :])
    k = each(lambda i: unit(k_ref[:, cols[i]].astype(F32)))
    plus = each(lambda i: jnp.exp(cum[i]))
    minus = each(lambda i: jnp.exp(-cum[i]))
    ending = each(lambda i: jnp.exp(last[i] - cum[i]))
    kp = each(lambda i: k[i][0] * plus[i])
    km = each(lambda i: k[i][0] * minus[i])
    ke = each(lambda i: k[i][0] * ending[i])
    beta = each(lambda i: column(beta_ref[...], base + i))
    end = each(lambda i: [end_ref[i]])
    upd = each(lambda i: split(upd_ref[i]))
    y = each(lambda i: y_ref[i] + mm(split(inv_ref[i]), split(mm(split(ke[i]), end[i])), 0, 0))
    rest_cot = each(lambda i: y[i] * beta[i])
    for i in range(count):
        vg_ref[:, cols[i]] = rest_cot[i].astype(BF)
    outer = each(lambda i: jnp.where(row > col, mm(split(y[i]), upd[i], 1, 1), 0.0))
    beta_cot = each(lambda i: jnp.sum(y[i] * rest_ref[i] - outer[i] * mix_ref[i], axis=1, keepdims=True))
    mix_cot = each(lambda i: split(-outer[i] * beta[i]))
    kp_cot = each(lambda i: mm(mix_cot[i], split(km[i]))
                  - mm(split(rest_cot[i]), split(start_ref[i]), 1, 1))
    km_cot = each(lambda i: mm(mix_cot[i], split(kp[i]), 0, 0) + kms_ref[i])
    ke_cot = each(lambda i: mm(upd[i], end[i], 1, 1))
    last_cot = each(lambda i: jnp.sum(ke_cot[i] * ke[i], axis=0, keepdims=True) + jnp.exp(last[i]) * sum(
        dot(ones, piece, 1, 1) for piece in split3(start_ref[i] * end_ref[i].astype(F32)))[0:1, :])
    cum_cot = each(lambda i: split3(
        term_ref[i] + kp_cot[i] * kp[i] - km_cot[i] * km[i] - ke_cot[i] * ke[i]))
    decay_cot = each(lambda i: sum(dot(upper, piece) for piece in cum_cot[i]) + last_cot[i])
    kn_cot = each(lambda i: kp_cot[i] * plus[i] + km_cot[i] * minus[i] + ke_cot[i] * ending[i])
    for i in range(count):
        kg_ref[:, cols[i]] = (k[i][1] * (
            kn_cot[i] - k[i][0] * jnp.sum(kn_cot[i] * k[i][0], axis=1, keepdims=True))).astype(BF)
    up = each(lambda i: up_ref[i])
    gate = each(lambda i: dot(low_ref[...], up[i]) + bias_ref[:, cols[i]])
    input_grad = each(lambda i: decay_cot[i] * -rate_ref[:, cols[i]] * jax.nn.sigmoid(gate[i]))
    half = each(lambda i: input_grad[i].astype(BF))
    for i in range(count):
        half_ref[i] = half[i]
        vec_ref[i] = jnp.concatenate([
            jnp.sum(input_grad[i], axis=0, keepdims=True),
            -jnp.sum(decay_cot[i] * softplus(gate[i]), axis=0, keepdims=True)], axis=0)
    low_acc[...] += sum(each(lambda i: dot(half[i], up[i], 1, 1)))
    score_acc[...] += sum(each(lambda i: jnp.where(
        col == base + i, beta_cot[i] * beta[i] * (1.0 - beta[i]), 0.0)))

    @pl.when(step == pl.num_programs(0) - 1)
    def _():
        lowg_ref[...] = low_acc[...].astype(BF)
        score_ref[...] = score_acc[...].T[0:score_ref.shape[0], :].astype(BF)


def weights_kernel(hid_ref, got_ref, out_ref, *, heads, rows):
    seqs = got_ref.shape[0]
    low_at = heads * N
    score_at = low_at + N
    down = jnp.zeros((rows, N), F32)
    beta = jnp.zeros((16, rows), F32)
    ups = [jnp.zeros((N, N), F32) for _ in range(heads)]
    vec = jnp.zeros((got_ref.shape[1] - score_at - 16, N), F32)
    for s in range(seqs):
        hid = hid_ref[s, 0:rows, :]
        rank = hid_ref[s, rows:rows + N, :]
        down = down + dot(hid, got_ref[s, low_at:low_at + N, :])
        beta = beta + dot(got_ref[s, score_at:score_at + 16, :], hid, 1, 1)
        for h in range(heads):
            ups[h] = ups[h] + dot(rank, got_ref[s, h * N:(h + 1) * N, :], 0, 0)
        vec = vec + got_ref[s, score_at + 16:, :].astype(F32)
    half = vec.shape[0] // 2
    at = 0
    for up in ups:
        out_ref[at:at + N, :] = up
        at += N
    out_ref[at:at + rows, :] = down
    at += rows
    out_ref[at:at + half, :] = vec[:half] + vec[half:]
    at += half
    for piece in range(0, rows, N):
        width = min(N, rows - piece)
        if width < N:
            out_ref[at:at + 16, :] = jnp.zeros((16, N), F32)
        out_ref[at:at + 16, 0:width] = beta[:, piece:piece + width]
        at += 16
    out_ref[at:, :] = jnp.zeros((out_ref.shape[0] - at, N), F32)


def call(kernel, name, **kw):
    return pl.pallas_call(kernel, interpret=INTERPRET, name=name,
                          compiler_params=pltpu.CompilerParams(vmem_limit_bytes=56 << 20), **kw)


def shape(dims, dtype):
    return jax.ShapeDtypeStruct(dims, dtype)


def on_device(nf, ny, nz, hidden, query_heads, key_heads, value_heads, out_grad, checkpoint,
              gate_down, gate_up, gate_bias, decay_rate, beta_weight):
    tok, width = hidden.shape[1], hidden.shape[2]
    heads = checkpoint.shape[2]
    inner = heads * N
    rows = width // nf
    own = heads // nf
    group = heads // nz
    hidden_rows = hidden.reshape(tok, width)

    beta_rows = rows * heads // N
    up_rows = own * N
    mine = jnp.concatenate([
        gate_up.reshape(N, own, N).swapaxes(0, 1).reshape(up_rows, N),
        gate_down,
        beta_weight.reshape(beta_rows, N)], axis=0)
    mine = jnp.pad(mine, ((0, -mine.shape[0] % 16), (0, 0)))
    got = lax.all_to_all(jnp.broadcast_to(mine[None], (nf,) + mine.shape), "fsdp", 0, 0, tiled=True)
    ups = got[:, :up_rows, :].reshape(heads, N, N)
    down_full = got[:, up_rows:up_rows + rows, :].reshape(width, N)
    beta_full = got[:, up_rows + rows:up_rows + rows + beta_rows, :].reshape(width, heads)

    low_rank = jnp.dot(hidden_rows, down_full, preferred_element_type=F32).astype(BF)
    beta_gate = jax.nn.sigmoid(jnp.dot(hidden_rows, beta_full, preferred_element_type=F32))
    bias = gate_bias.reshape(1, inner)
    rate = decay_rate.reshape(1, inner)
    q, k, v, g = (x.reshape(tok, inner) for x in (query_heads, key_heads, value_heads, out_grad))
    start = checkpoint.reshape(heads, N, N)

    whole = lambda dims: pl.BlockSpec(dims, lambda i: (0,) * len(dims))
    row_spec = lambda hb: pl.BlockSpec((1, hb * N), lambda i: (0, i))
    tok_spec = lambda hb: pl.BlockSpec((N, hb * N), lambda i: (0, i))
    mat_spec = lambda hb: pl.BlockSpec((hb, N, N), lambda i: (i, 0, 0))
    gate_specs = lambda hb: [
        whole((tok, N)), mat_spec(hb), row_spec(hb), row_spec(hb), whole((tok, heads))]
    gate_args = (low_rank, ups, bias, rate, beta_gate)
    mat = shape((heads, N, N), F32)
    cost = pl.CostEstimate(flops=4 * 10**9, bytes_accessed=12 << 20, transcendentals=0)

    hb = FIRST_HB
    send, inv, mix, sco, cum = call(
        first_kernel, "first",
        grid=(heads // hb,),
        in_specs=gate_specs(hb) + [tok_spec(hb)] * 3,
        out_specs=[pl.BlockSpec((hb, 2 * N, N), lambda i: (i, 0, 0))] + [mat_spec(hb)] * 4,
        out_shape=[shape((heads, 2 * N, N), BF)] + [mat] * 4,
    )(*gate_args, q, k, g)

    spread = lax.all_to_all(send, "z", 0, 0, tiled=True).reshape(nz, group, 2 * N, N)

    hb = HB
    q_grad, rest, upd, y, kms, term = call(
        middle_kernel, "middle",
        grid=(heads // hb,),
        in_specs=[whole((tok, heads))] + [tok_spec(hb)] * 4 + [mat_spec(hb)] * 4,
        out_specs=[tok_spec(hb)] + [mat_spec(hb)] * 5,
        out_shape=[shape((tok, inner), BF)] + [mat] * 5,
        cost_estimate=cost,
    )(beta_gate, q, k, v, g, start, inv, sco, cum)

    every, total = call(
        chain_kernel, "chain",
        out_shape=[shape((nz, group, N, 2 * N), F32), shape((group, N, 2 * N), BF)],
    )(spread)
    later = [lax.ppermute(total, "y", [(y + d, y) for y in range(ny - d)])
             for d in range(ny - 1, 0, -1)]
    end = call(apply_kernel, "apply", out_shape=shape((nz, group, N, N), BF))(every, *later)
    end = lax.all_to_all(end.reshape(heads, N, N), "z", 0, 0, tiled=True)

    early = jnp.concatenate([
        hidden_rows.T.reshape(nf, rows, tok),
        jnp.broadcast_to(low_rank[None], (nf, tok, N))], axis=1)
    end, early = lax.optimization_barrier((end, early))
    early = lax.all_to_all(early, "fsdp", 0, 0, tiled=True)

    k_grad, v_grad, half, vec, low_grad, score = call(
        second_kernel, "second",
        grid=(heads // hb,),
        in_specs=gate_specs(hb) + [tok_spec(hb)] + [mat_spec(hb)] * 10,
        out_specs=[tok_spec(hb)] * 2 + [
            mat_spec(hb), pl.BlockSpec((hb, 2, N), lambda i: (i, 0, 0)),
            whole((N, N)), whole((heads, N))],
        out_shape=[shape((tok, inner), BF)] * 2 + [
            shape((heads, N, N), BF), shape((heads, 2, N), F32),
            shape((N, N), BF), shape((heads, N), BF)],
        scratch_shapes=[pltpu.VMEM((N, N), F32)] * 2,
        cost_estimate=cost,
    )(*gate_args, k, start, end, inv, mix, cum, rest, upd, y, kms, term)

    vec = vec.reshape(2 * heads, N)
    vec_hi = vec.astype(BF)
    vec_lo = (vec - vec_hi.astype(F32)).astype(BF)
    common = jnp.concatenate([low_grad, score, vec_hi, vec_lo], axis=0)
    terms = jnp.concatenate([
        half.reshape(nf, own * N, N),
        jnp.broadcast_to(common[None], (nf,) + common.shape)], axis=1)
    terms = lax.all_to_all(terms, "fsdp", 0, 0, tiled=True)
    beta_out = 16 * -(-rows // N)
    used = own * N + rows + 2 * heads + beta_out
    parts = ny * nz
    chunk = 8 * -(-used // (8 * parts))
    sums = call(
        functools.partial(weights_kernel, heads=own, rows=rows), "weights",
        out_shape=shape((parts * chunk, N), F32),
    )(early, terms)
    sums = lax.all_to_all(sums.reshape(parts, chunk, N), ("y", "z"), 0, 0, tiled=True)
    sums = jnp.broadcast_to(jnp.sum(sums, axis=0)[None], (parts, chunk, N))
    sums = lax.all_to_all(sums, ("y", "z"), 0, 0, tiled=True).reshape(parts * chunk, N)
    at = own * N
    up_grad = sums[:at].reshape(own, N, N).swapaxes(0, 1).reshape(N, own * N)
    down_grad = sums[at:at + rows]
    at += rows
    vectors = sums[at:at + 2 * heads].reshape(heads, 2, N).swapaxes(0, 1).reshape(2, inner)
    at += 2 * heads
    beta_grad = sums[at:at + beta_out].reshape(-1, 16, N).swapaxes(0, 1).reshape(16, -1)
    beta_grad = beta_grad[:, :rows].T

    hidden_grad = (
        lax.dot_general(low_grad, down_full, (((1,), (1,)), ((), ())), preferred_element_type=F32)
        + lax.dot_general(score, beta_full, (((0,), (1,)), ((), ())), preferred_element_type=F32)
    ).astype(BF)

    return (q_grad[None], k_grad[None], v_grad[None], hidden_grad[None],
            down_grad, up_grad, beta_grad, vectors[0], vectors[1])


def grid_of(size):
    ny = 1
    while ny * ny * 4 <= size:
        ny *= 2
    return ny, size // ny


def solution(mesh):
    nf, size = mesh.shape["fsdp"], mesh.shape["ctx"]
    ny, nz = grid_of(size)
    fine = Mesh(mesh.devices.reshape(nf, ny, nz), ("fsdp", "y", "z"))
    ctx = ("y", "z")
    tokens = P("fsdp", ctx, None)
    return jax.shard_map(
        functools.partial(on_device, nf, ny, nz),
        mesh=fine,
        in_specs=(tokens,) * 5 + (
            P("fsdp", ctx, None, None, None), P("fsdp", None), P(None, "fsdp"), P(), P(),
            P("fsdp", None)),
        out_specs=(tokens,) * 4 + (
            P("fsdp", None), P(None, "fsdp"), P("fsdp", None), P(), P()),
        check_vma=False,
    )
```

time: 1270 us -> 199 us (0.16); the launches traced: 1250 us -> 197 us
  waiting for transfers between devices: 497 us -> 28.4 us
  other arithmetic: 199 us -> 4.58 us
  matrix products: 182 us -> 3.35 us
  local copies, waits for them, and re-layouts: 159 us -> 7.8 us
  blocking collectives: 202 us -> 96.4 us
  Pallas kernels: 0 us -> 38.3 us
  starting transfers between devices: 0.43 us -> 17.9 us
  between operations: 15.1 us -> 0.83 us
    all_gather x2 -> x0, waiting for transfers between devices: 410 us -> none  [carried_in(): pieces = jax.tree.map(lambda part: lax.all_gather(part, axis), value)]
    another operation x8 -> x0, other arithmetic: 191 us -> none  [the longest x5 163 us: block_advance(): jax.scipy.linalg.solve_triangular(system, target, lower=True, unit_diagon...]
    dot_general x59 -> x4, matrix products: 171 us -> 3.35 us  [the longest x1 1.18 us: on_device(): lax.dot_general(score, beta_full, (((0,), (1,)), ((), ())), preferred_ele...]
    psum x2 -> x0, blocking collectives: 162 us -> none  [the longest x1 138 us: on_device(): lax.psum((down_term, beta_term, up_term, bias_term, rate_term), 'ctx')]
    all_to_all x0 -> x4, blocking collectives: none -> 96.4 us  [the longest x1 35.7 us: on_device(): lax.all_to_all(send, 'z', 0, 0, tiled=True).reshape(nz, group, 2 * N, N)]
    unnamed x8 -> x0, waiting for transfers between devices: 53 us -> none
    rev x2 -> x0, local copies, waits for them, and re-layouts: 46.4 us -> none  [carried_in(): pieces = jax.tree.map(lambda part: part[::-1], pieces)]
    all_gather x3 -> x0, blocking collectives: 39.9 us -> none  [the longest x1 13.6 us: on_device(): lax.all_gather(gate_down, 'fsdp', axis=0, tiled=True)]
  transfers between devices with their start and end apart: 6 -> 6, of which waited for: 5 -> 6; matrix products, arithmetic and copies ran while one was open for 6% -> 3% of each run, Pallas kernels for 0% -> 9%
where the time goes in v1:
time: 199 us; the launch traced here: 197 us
  blocking collectives  96.4 us (48%)
  Pallas kernels  38.3 us (19%)
  waiting for transfers between devices  28.4 us (14%)
  starting transfers between devices  17.9 us (9%)
  local copies, waits for them, and re-layouts  7.8 us (4%)
  other arithmetic  4.58 us (2%)
  matrix products  3.35 us (2%)
    all_to_all x1, blocking collectives, on_device(): lax.all_to_all(send, 'z', 0, 0, tiled=True).reshape(nz, group, 2 * N, N)  35.7 us
    all_to_all x1, blocking collectives, on_device(): lax.all_to_all(jnp.broadcast_to(mine[None], (nf,) + mine.shape), 'fsdp',...  22 us
    all_to_all x1, blocking collectives, on_device(): lax.all_to_all(sums.reshape(parts, chunk, N), ('y', 'z'), 0, 0, tiled=True)  20.1 us
    all_to_all x1, blocking collectives, on_device(): terms = lax.all_to_all(terms, 'fsdp', 0, 0, tiled=True)  18.6 us
    all_to_all x1, waiting for transfers between devices, on_device(): lax.all_to_all(sums, ('y', 'z'), 0, 0, tiled=True).reshape(parts * chunk, N)  13.1 us
    pallas_call x1, Pallas kernels, on_device(): call(first_kernel, 'first', grid=(heads // hb,), in_specs=gate_specs(hb)...  10.2 us
    pallas_call x1, Pallas kernels, on_device(): call(second_kernel, 'second', grid=(heads // hb,), in_specs=gate_specs(hb...  10.1 us
    ppermute x3, waiting for transfers between devices, on_device(): lax.ppermute(total, 'y', [(y + d, y) for y in range(ny - d)])  9.06 us
  transfers between devices with their start and end apart: 6, of which 6 were waited for; matrix products, arithmetic and copies ran while one was open for 3% of the time, Pallas kernels for 9%

profile of v1, /device:TPU:32, one launch (start us, length us, event | category | flops | bytes accessed | tf_op | source)
XLA Modules:
  0.0 197.5 jit_solution(2601849912437205145)
XLA Ops:
  0.6 0.9 reshape.107
  1.5 0.8 copy.33
  2.4 0.1 reshape.109
  2.5 0.9 fusion.13
  3.4 0.2 broadcast_in_dim.16
  3.5 0.0 copy-start
  3.6 22.0 %all_to_all.35 = bf16[8,592,128]{2,1,0:T(8,128)(2,1)S(1)} all-to-all(bf16[8,592,128]{2,1,0:T(8,128)(2,1)S(1)} %broadcast_in_dim.16), channel_id=1, replica_groups=mesh['fsdp'=8,'y'=4,'z'=8] {'fsdp'}, dimensions={0} | all-to-all | bytes 2424832 | tf_op jit(solution)/shard_map/all_to_all | solution.py:330
  25.5 0.4 reshape.110
  25.9 0.0 copy-done
  25.9 0.9 fusion.5.beta_ref
  26.9 0.9 fusion.6.low_ref
  27.9 0.8 slice.45
  28.7 10.2 %first.1 = (bf16[16,256,128]{2,1,0:T(8,128)(2,1)}, f32[16,128,128]{2,1,0:T(8,128)}, f32[16,128,128]{2,1,0:T(8,128)}, f32[16,128,128]{2,1,0:T(8,128)}, f32[16,128,128]{2,1,0:T(8,128)}) custom-call(bf16[128,128]{1,0:T(8,128)(2,1)} %fusion.6.low_ref, bf16[16,128,128]{2,1,0:T(8,128)(2,1)} %bitcast.65, f32[1,2048]{1,0:T(1,128)} %bitcast.89, f32[1,2048]{1,0:T(1,128)} %bitcast.91, ...), custom_call_target="tpu_custom_call" | custom-call | tf_op jit(solution)/shard_map/first/pallas_call | solution.py:353
  38.9 35.7 %all_to_all.36 = bf16[16,256,128]{2,1,0:T(8,128)(2,1)} all-to-all(bf16[16,256,128]{2,1,0:T(8,128)(2,1)} %get-tuple-element.34), channel_id=1, replica_groups=mesh['fsdp'=8,'y'=4,'z'=8] {'z'}, dimensions={0} | all-to-all | bytes 2097152 | tf_op jit(solution)/shard_map/all_to_all | solution.py:361
  74.6 4.0 %chain.1 = (f32[8,2,128,256]{3,2,1,0:T(8,128)}, bf16[2,128,256]{2,1,0:T(8,128)(2,1)}) custom-call(bf16[8,2,256,128]{3,2,1,0:T(8,128)(2,1)} %bitcast.63), custom_call_target="tpu_custom_call" | custom-call | tf_op jit(solution)/shard_map/chain/pallas_call | solution.py:373
  78.6 1.3 collective-permute-start.2
  79.9 1.3 collective-permute-start.1
  81.2 1.3 collective-permute-start
  82.5 3.2 %collective-permute-done.2.refs_2_ = bf16[2,128,256]{2,1,0:T(8,128)(2,1)S(1)} collective-permute-done((bf16[2,128,256]{2,1,0:T(8,128)(2,1)}, bf16[2,128,256]{2,1,0:T(8,128)(2,1)S(1)}, u32[]{:S(2)}, u32[]{:S(2)}) %collective-permute-start.2) | collective-permute-done | bytes 131104 | tf_op jit(solution)/shard_map/ppermute | solution.py:377
  85.7 0.0 copy-start.4
  85.7 3.0 %collective-permute-done.1.refs_1_ = bf16[2,128,256]{2,1,0:T(8,128)(2,1)S(1)} collective-permute-done((bf16[2,128,256]{2,1,0:T(8,128)(2,1)}, bf16[2,128,256]{2,1,0:T(8,128)(2,1)S(1)}, u32[]{:S(2)}, u32[]{:S(2)}) %collective-permute-start.1) | collective-permute-done | bytes 131104 | tf_op jit(solution)/shard_map/ppermute | solution.py:377
  88.7 0.0 copy-start.5
  88.7 2.9 %collective-permute-done.refs_0_ = bf16[2,128,256]{2,1,0:T(8,128)(2,1)S(1)} collective-permute-done((bf16[2,128,256]{2,1,0:T(8,128)(2,1)}, bf16[2,128,256]{2,1,0:T(8,128)(2,1)S(1)}, u32[]{:S(2)}, u32[]{:S(2)}) %collective-permute-start) | collective-permute-done | bytes 131104 | tf_op jit(solution)/shard_map/ppermute | solution.py:377
  91.6 0.0 copy-start.6
  91.6 0.0 copy-done.4
  91.6 0.0 copy-done.5
  91.6 0.6 copy-done.6
  92.3 3.4 %apply.1 = bf16[8,2,128,128]{3,2,1,0:T(8,128)(2,1)} custom-call(f32[8,2,128,256]{3,2,1,0:T(8,128)} %get-tuple-element.35.all_ref, bf16[2,128,256]{2,1,0:T(8,128)(2,1)} %copy-done.6, bf16[2,128,256]{2,1,0:T(8,128)(2,1)} %copy-done.5, bf16[2,128,256]{2,1,0:T(8,128)(2,1)} %copy-done.4), custom_call_target="tpu_custom_call" | custom-call | tf_op jit(solution)/shard_map/apply/pallas_call | solution.py:379
  95.6 0.0 copy-start.2
  95.6 5.0 %all-to-all-start.2 = ((bf16[16,128,128]{2,1,0:T(8,128)(2,1)}), bf16[16,128,128]{2,1,0:T(8,128)(2,1)S(1)}, u32[]{:S(2)}, u32[]{:S(2)}) async-start(bf16[16,128,128]{2,1,0:T(8,128)(2,1)} %bitcast.67), calls=%async_computation.2 | async-start | bytes 1048576 | tf_op jit(solution)/shard_map/all_to_all | solution.py:380
  100.6 0.3 copy.38
  100.9 0.0 copy-done.2
  101.0 0.9 pad_maximum_fusion.1
  101.9 7.7 %middle.1 = (bf16[128,2048]{1,0:T(8,128)(2,1)}, f32[16,128,128]{2,1,0:T(8,128)}, f32[16,128,128]{2,1,0:T(8,128)}, f32[16,128,128]{2,1,0:T(8,128)}, f32[16,128,128]{2,1,0:T(8,128)}, /*index=5*/f32[16,128,128]{2,1,0:T(8,128)}) custom-call(f32[128,16]{1,0:T(8,128)} %fusion.5.beta_ref, bf16[128,2048]{1,0:T(8,128)(2,1)} %bitcast.75, bf16[128,2048]{1,0:T(8,128)(2,1)} %bitcast.79, ...), custom_call_target="tpu_custom_call" | custom-call | flops 4000000000 | bytes 12582912 | tf_op jit(solution)/shard_map/middle/pallas_call | solution.py:364
  109.7 5.3 %all-to-all-done.2.end_ref = bf16[16,128,128]{2,1,0:T(8,128)(2,1)S(1)} async-done(((bf16[16,128,128]{2,1,0:T(8,128)(2,1)}), bf16[16,128,128]{2,1,0:T(8,128)(2,1)S(1)}, u32[]{:S(2)}, u32[]{:S(2)}) %all-to-all-start.2) | async-done | bytes 524320 | tf_op jit(solution)/shard_map/all_to_all | solution.py:380
  115.0 0.0 copy-start.1
  115.0 4.2 %all-to-all-start.3 = ((bf16[8,416,128]{2,1,0:T(8,128)(2,1)}), bf16[8,416,128]{2,1,0:T(8,128)(2,1)}, u32[]{:S(2)}, u32[]{:S(2)}) async-start(bf16[8,416,128]{2,1,0:T(8,128)(2,1)} %pad_maximum_fusion.1), calls=%async_computation.3 | async-start | bytes 1703936 | tf_op jit(solution)/shard_map/all_to_all | solution.py:386
  119.2 0.0 copy-done.1
  119.2 10.1 %second.1 = (bf16[128,2048]{1,0:T(8,128)(2,1)}, bf16[128,2048]{1,0:T(8,128)(2,1)}, bf16[16,128,128]{2,1,0:T(8,128)(2,1)}, f32[16,2,128]{2,1,0:T(2,128)}, bf16[12...) custom-call(bf16[128,128]{1,0:T(8,128)(2,1)} %fusion.6.low_ref, bf16[16,128,128]{2,1,0:T(8,128)(2,1)} %bitcast.66, ...), custom_call_target="tpu_custom_call" | custom-call | flops 4000000000 | bytes 12582912 | tf_op jit(solution)/shard_map/second/pallas_call | solution.py:388
  129.4 0.8 subtract_convert_fusion
  130.2 0.8 pad_maximum_fusion.2
  131.0 0.1 broadcast_in_dim.42
  131.0 1.1 pad_maximum_fusion
  132.1 0.9 all-to-all-done.3.hid_ref
  133.1 18.6 %all_to_all.37.got_ref = bf16[8,464,128]{2,1,0:T(8,128)(2,1)} all-to-all(bf16[8,464,128]{2,1,0:T(8,128)(2,1)S(1)} %pad_maximum_fusion), channel_id=1, replica_groups=mesh['fsdp'=8,'y'=4,'z'=8] {'fsdp'}, dimensions={0} | all-to-all | bytes 1900544 | tf_op jit(solution)/shard_map/all_to_all | solution.py:409
  151.6 2.8 %weights.1 = f32[768,128]{1,0:T(8,128)} custom-call(bf16[8,416,128]{2,1,0:T(8,128)(2,1)} %all-to-all-done.3.hid_ref, bf16[8,464,128]{2,1,0:T(8,128)(2,1)} %all_to_all.37.got_ref), custom_call_target="tpu_custom_call" | custom-call | tf_op jit(solution)/shard_map/weights/pallas_call | solution.py:414
  154.4 0.0 copy-start.3
  154.4 20.1 %all_to_all.38 = f32[32,24,128]{2,1,0:T(8,128)S(1)} all-to-all(f32[32,24,128]{2,1,0:T(8,128)} %bitcast.68), channel_id=1, replica_groups=mesh['fsdp'=8,'y'=4,'z'=8] {'y','z'}, dimensions={0} | all-to-all | bytes 786432 | tf_op jit(solution)/shard_map/all_to_all | solution.py:418
  174.6 0.0 copy-start.7
  174.6 0.8 broadcast_in_dim.43
  175.4 4.8 %all-to-all-start.6 = ((f32[32,24,128]{2,1,0:T(8,128)}), f32[32,24,128]{2,1,0:T(8,128)S(1)}, u32[]{:S(2)}, u32[]{:S(2)}) async-start(f32[32,24,128]{2,1,0:T(8,128)} %broadcast_in_dim.43), calls=%async_computation.6 | async-start | bytes 786432 | tf_op jit(solution)/shard_map/all_to_all | solution.py:420
  180.2 0.0 copy-done.3
  180.2 0.3 fusion.15
  180.5 0.0 copy-done.7
  180.5 1.2 fusion.1
  181.7 13.1 %all-to-all-done.6 = f32[32,24,128]{2,1,0:T(8,128)S(1)} async-done(((f32[32,24,128]{2,1,0:T(8,128)}), f32[32,24,128]{2,1,0:T(8,128)S(1)}, u32[]{:S(2)}, u32[]{:S(2)}) %all-to-all-start.6) | async-done | bytes 393248 | tf_op jit(solution)/shard_map/all_to_all | solution.py:420
  194.8 0.7 slice.46
  195.5 0.6 fusion.14
  196.1 0.6 slice_bitcast_fusion
  196.7 0.1 copy.39
  196.8 0.7 copy.47
  (9 shorter events, 0.2 us)
Async XLA Ops:
  3.5 22.4 %copy-start = (bf16[1,128,2304]{2,1,0:T(8,128)(2,1)S(1)}, bf16[1,128,2304]{2,1,0:T(8,128)(2,1)}, u32[]{:S(2)}) copy-start(bf16[1,128,2304]{2,1,0:T(8,128)(2,1)} %param.11) | copy-start | bytes 1769476
  78.6 7.1 %collective-permute-start.2 = (bf16[2,128,256]{2,1,0:T(8,128)(2,1)}, bf16[2,128,256]{2,1,0:T(8,128)(2,1)S(1)}, u32[]{:S(2)}, u32[]{:S(2)}) collective-permute-start(bf16[2,128,256]{2,1,0:T(8,128)(2,1)} %get-tuple-element.36), channel_id=1, source_target_pairs={{8,0},{16,8},{24,16},{9,1},{17,9},{25,17},{10,2},{18,10},{26,18},{... | collective-permute-start | bytes 393224 | tf_op jit(solution)/shard_map/ppermute | solution.py:377
  79.9 8.8 %collective-permute-start.1 = (bf16[2,128,256]{2,1,0:T(8,128)(2,1)}, bf16[2,128,256]{2,1,0:T(8,128)(2,1)S(1)}, u32[]{:S(2)}, u32[]{:S(2)}) collective-permute-start(bf16[2,128,256]{2,1,0:T(8,128)(2,1)} %get-tuple-element.36), channel_id=1, source_target_pairs={{16,0},{24,8},{17,1},{25,9},{18,2},{26,10},{19,3},{27,11},{20,4},{... | collective-permute-start | bytes 393224 | tf_op jit(solution)/shard_map/ppermute | solution.py:377
  81.2 10.4 %collective-permute-start = (bf16[2,128,256]{2,1,0:T(8,128)(2,1)}, bf16[2,128,256]{2,1,0:T(8,128)(2,1)S(1)}, u32[]{:S(2)}, u32[]{:S(2)}) collective-permute-start(bf16[2,128,256]{2,1,0:T(8,128)(2,1)} %get-tuple-element.36), channel_id=1, source_target_pairs={{24,0},{25,1},{26,2},{27,3},{28,4},{29,5},{30,6},{31,7},{56,32},{5... | collective-permute-start | bytes 393224 | tf_op jit(solution)/shard_map/ppermute | solution.py:377
  85.7 5.9 %copy-start.4 = (bf16[2,128,256]{2,1,0:T(8,128)(2,1)}, bf16[2,128,256]{2,1,0:T(8,128)(2,1)S(1)}, u32[]{:S(2)}) copy-start(bf16[2,128,256]{2,1,0:T(8,128)(2,1)S(1)} %collective-permute-done.2.refs_2_) | copy-start | bytes 393220
  88.7 2.9 %copy-start.5 = (bf16[2,128,256]{2,1,0:T(8,128)(2,1)}, bf16[2,128,256]{2,1,0:T(8,128)(2,1)S(1)}, u32[]{:S(2)}) copy-start(bf16[2,128,256]{2,1,0:T(8,128)(2,1)S(1)} %collective-permute-done.1.refs_1_) | copy-start | bytes 393220
  91.6 0.7 copy-start.6
  95.6 5.3 %copy-start.2 = (bf16[128,128]{1,0:T(8,128)(2,1)S(1)}, bf16[128,128]{1,0:T(8,128)(2,1)}, u32[]{:S(2)}) copy-start(bf16[128,128]{1,0:T(8,128)(2,1)} %fusion.6.low_ref) | copy-start | bytes 98308
  95.6 19.4 %all-to-all-start.2 = ((bf16[16,128,128]{2,1,0:T(8,128)(2,1)}), bf16[16,128,128]{2,1,0:T(8,128)(2,1)S(1)}, u32[]{:S(2)}, u32[]{:S(2)}) async-start(bf16[16,128,128]{2,1,0:T(8,128)(2,1)} %bitcast.67), calls=%async_computation.2 | async-start | bytes 1048576 | tf_op jit(solution)/shard_map/all_to_all | solution.py:380
  115.0 4.2 %copy-start.1 = (bf16[16,128,128]{2,1,0:T(8,128)(2,1)}, bf16[16,128,128]{2,1,0:T(8,128)(2,1)S(1)}, u32[]{:S(2)}) copy-start(bf16[16,128,128]{2,1,0:T(8,128)(2,1)S(1)} %all-to-all-done.2.end_ref) | copy-start | bytes 1572868
  115.0 18.1 %all-to-all-start.3 = ((bf16[8,416,128]{2,1,0:T(8,128)(2,1)}), bf16[8,416,128]{2,1,0:T(8,128)(2,1)}, u32[]{:S(2)}, u32[]{:S(2)}) async-start(bf16[8,416,128]{2,1,0:T(8,128)(2,1)} %pad_maximum_fusion.1), calls=%async_computation.3 | async-start | bytes 1703936 | tf_op jit(solution)/shard_map/all_to_all | solution.py:386
  154.4 25.8 %copy-start.3 = (bf16[128,128]{1,0:T(8,128)(2,1)S(1)}, bf16[128,128]{1,0:T(8,128)(2,1)}, u32[]{:S(2)}) copy-start(bf16[128,128]{1,0:T(8,128)(2,1)} %get-tuple-element.46) | copy-start | bytes 98308
  174.6 5.9 %copy-start.7 = (bf16[16,128]{1,0:T(8,128)(2,1)S(1)}, bf16[16,128]{1,0:T(8,128)(2,1)}, u32[]{:S(2)}) copy-start(bf16[16,128]{1,0:T(8,128)(2,1)} %get-tuple-element.47) | copy-start | bytes 12292
  175.4 19.4 %all-to-all-start.6 = ((f32[32,24,128]{2,1,0:T(8,128)}), f32[32,24,128]{2,1,0:T(8,128)S(1)}, u32[]{:S(2)}, u32[]{:S(2)}) async-start(f32[32,24,128]{2,1,0:T(8,128)} %broadcast_in_dim.43), calls=%async_computation.6 | async-start | bytes 786432 | tf_op jit(solution)/shard_map/all_to_all | solution.py:420

commit v2 on v1

--- a/solution.py
+++ b/solution.py
@@ -13,6 +13,9 @@
 N = 128
 HB = 4
 FIRST_HB = 8
+LINK = jnp.bfloat16
+RUN = 4
+MIB = 28
 INTERPRET = False
 
 
@@ -93,6 +96,53 @@
     return [slice(i * N, (i + 1) * N) for i in range(count)]
 
 
+def pad_to_square(x):
+    if x.shape[0] < N:
+        x = jnp.concatenate([x, jnp.zeros((N - x.shape[0], x.shape[1]), x.dtype)], axis=0)
+    if x.shape[1] < N:
+        x = jnp.concatenate([x, jnp.zeros((N, N - x.shape[1]), x.dtype)], axis=1)
+    return x
+
+
+def widen(x):
+    if x.shape[1] == N:
+        return x
+    return jnp.concatenate([x, jnp.zeros((x.shape[0], N - x.shape[1]), x.dtype)], axis=1)
+
+
+def pack_kernel(up_ref, down_ref, beta_ref, out_ref):
+    rows = beta_ref.shape[1]
+    parts = [up_ref[:, a:a + N] for a in range(0, up_ref.shape[1], N)] + [down_ref[...]]
+    parts += [widen(beta_ref[:, a:min(a + N, rows)]) for a in range(0, rows, N)]
+    mine = jnp.concatenate(parts, axis=0)
+    for r in range(out_ref.shape[0]):
+        out_ref[r] = mine
+
+
+def arrange_kernel(core_ref, ours_ref, theirs_ref, hidden_ref, turned_ref,
+                   up_ref, down_ref, betas_ref, low_ref, gate_ref, *, rows):
+    pairs = ours_ref.shape[0]
+    heads = gate_ref.shape[1]
+    own = up_ref.shape[0] // (2 * pairs)
+    core = core_ref[0]
+    logits = jnp.zeros((heads, N), F32)
+    for ref, place in ((ours_ref, core), (theirs_ref, 1 - core)):
+        for x in range(pairs):
+            owner = 2 * x + place
+            for h in range(own):
+                up_ref[owner * own + h] = ref[x, h * N:(h + 1) * N, :]
+            down_ref[pl.ds(pl.multiple_of(owner * rows, 16), rows), :] = ref[x, own * N:own * N + rows, :]
+            at = own * N + rows
+            betas_ref[owner] = ref[x, at:, :]
+            for a in range(0, rows, N):
+                size = min(N, rows - a)
+                start = pl.multiple_of(owner * rows + a, 16)
+                logits += dot(ref[x, at:at + heads, 0:size], turned_ref[pl.ds(start, size), :])
+                at += heads
+    low_ref[...] = dot(hidden_ref[...], down_ref[...]).astype(BF)
+    gate_ref[...] = jax.nn.sigmoid(pad_to_square(logits).T[:, 0:heads])
+
+
 def first_kernel(low_ref, up_ref, bias_ref, rate_ref, beta_ref, q_ref, k_ref, g_ref,
                  send_ref, inv_ref, mix_ref, sco_ref, cum_ref):
     count = inv_ref.shape[0]
@@ -132,40 +182,48 @@
         send_ref[i, N:2 * N, :] = local[i].astype(BF)
 
 
-def chain_kernel(got_ref, all_ref, tot_ref):
-    blocks, heads = got_ref.shape[0], got_ref.shape[1]
-    each = lambda f: [f(h) for h in range(heads)]
-    both = each(lambda h: jnp.concatenate(
-        [got_ref[blocks - 1, h, 0:N, :], got_ref[blocks - 1, h, N:2 * N, :]], axis=1).astype(F32))
-    for j in range(blocks - 1, -1, -1):
-        if j < blocks - 1:
-            both = each(lambda h: mm([got_ref[j, h, 0:N, :]], split(both[h])))
-            both = each(lambda h: jnp.concatenate(
-                [both[h][:, :N], both[h][:, N:] + got_ref[j, h, N:2 * N, :].astype(F32)], axis=1))
-        for h in range(heads):
-            all_ref[j, h] = both[h]
-    for h in range(heads):
-        tot_ref[h] = both[h].astype(BF)
-
-
-def apply_kernel(all_ref, *refs):
-    *later, end_ref = refs
-    blocks, heads = all_ref.shape[0], all_ref.shape[1]
-    each = lambda f: [f(h) for h in range(heads)]
-    carry = each(lambda h: jnp.zeros((N, N), F32))
-    for ref in later:
-        carry = each(lambda h: mm([ref[h, :, 0:N]], split(carry[h])) + ref[h, :, N:2 * N].astype(F32))
-    for h in range(heads):
-        end_ref[blocks - 1, h] = carry[h].astype(BF)
-    carry = each(lambda h: split(carry[h]))
+def chain_kernel(got_ref, map_ref, sum_ref, tot_ref):
+    blocks = got_ref.shape[0]
+    run = min(RUN, blocks)
+    starts = range(0, blocks, run)
+    local = {}
+    for a in starts:
+        last = a + run - 1
+        local[last] = jnp.concatenate(
+            [got_ref[last, 0:N, :], got_ref[last, N:2 * N, :]], axis=1).astype(F32)
+    for back in range(run - 2, -1, -1):
+        for a in starts:
+            both = mm([got_ref[a + back, 0:N, :]], split(local[a + back + 1]))
+            local[a + back] = jnp.concatenate(
+                [both[:, :N], both[:, N:] + got_ref[a + back, N:2 * N, :].astype(F32)], axis=1)
+
+    def after(one, total):
+        both = mm(split(one[:, :N]), total)
+        return jnp.concatenate([both[:, :N], both[:, N:] + one[:, N:]], axis=1)
+
+    totals = {}
+    for a in reversed(starts):
+        if a + run < blocks:
+            local[a] = after(local[a], totals[a + run])
+        totals[a] = split(local[a])
+    tot_ref[...] = local[0][:, N:].astype(BF)
+    for a in starts:
+        for j in range(a, a + run):
+            both = local[j] if j == a or a + run == blocks else after(local[j], totals[a + run])
+            map_ref[j] = both[:, :N].astype(BF)
+            sum_ref[j] = both[:, N:]
+
+
+def apply_kernel(map_ref, sum_ref, later_ref, end_ref):
+    blocks = map_ref.shape[0]
+    later = later_ref[...]
+    end_ref[blocks - 1] = later
     for j in range(blocks - 1):
-        for h in range(heads):
-            end_ref[j, h] = (mm(split(all_ref[j + 1, h, :, :N]), carry[h])
-                             + all_ref[j + 1, h, :, N:]).astype(BF)
-
-
-def middle_kernel(beta_ref, q_ref, k_ref, v_ref, g_ref, start_ref, inv_ref, sco_ref, cum_ref,
-                  qg_ref, rest_ref, upd_ref, y_ref, kms_ref, term_ref):
+        end_ref[j] = (dot(map_ref[j + 1], later) + sum_ref[j + 1]).astype(BF)
+
+
+def middle_kernel(low_ref, up_ref, bias_ref, rate_ref, beta_ref, q_ref, k_ref, v_ref, g_ref, start_ref, inv_ref, sco_ref, cum_ref,
+                  qg_ref, rest_ref, upd_ref, y_ref, kms_ref, term_ref, soft_ref, slope_ref):
     count = inv_ref.shape[0]
     base = pl.program_id(0) * count
     row, col = iotas()
@@ -195,13 +253,17 @@
         y_ref[i] = y[i]
         kms_ref[i] = kms[i]
         term_ref[i] = qp_cot[i] * qp[i]
-        qg_ref[:, i * N:(i + 1) * N] = (q[i][1] * (
+    gate = each(lambda i: dot(low_ref[...], up_ref[i]) + bias_ref[:, cols[i]])
+    for i in range(count):
+        soft_ref[i] = softplus(gate[i])
+        slope_ref[i] = -rate_ref[:, cols[i]] * jax.nn.sigmoid(gate[i])
+        qg_ref[:, cols[i]] = (q[i][1] * (
             qn_cot[i] - q[i][0] * jnp.sum(qn_cot[i] * q[i][0], axis=1, keepdims=True))).astype(BF)
 
 
-def second_kernel(low_ref, up_ref, bias_ref, rate_ref, beta_ref, k_ref, start_ref, end_ref,
+def second_kernel(core_ref, up_ref, beta_ref, k_ref, start_ref, end_ref,
                   inv_ref, mix_ref, cum_ref, rest_ref, upd_ref, y_ref, kms_ref, term_ref,
-                  kg_ref, vg_ref, half_ref, vec_ref, lowg_ref, score_ref, low_acc, score_acc):
+                  soft_ref, slope_ref, kg_ref, vg_ref, keep_ref, give_ref, lowg_ref, score_ref, low_acc, score_acc, vec_acc):
     count = inv_ref.shape[0]
     step = pl.program_id(0)
     base = step * count
@@ -249,61 +311,86 @@
         kg_ref[:, cols[i]] = (k[i][1] * (
             kn_cot[i] - k[i][0] * jnp.sum(kn_cot[i] * k[i][0], axis=1, keepdims=True))).astype(BF)
     up = each(lambda i: up_ref[i])
-    gate = each(lambda i: dot(low_ref[...], up[i]) + bias_ref[:, cols[i]])
-    input_grad = each(lambda i: decay_cot[i] * -rate_ref[:, cols[i]] * jax.nn.sigmoid(gate[i]))
+    input_grad = each(lambda i: decay_cot[i] * slope_ref[i])
     half = each(lambda i: input_grad[i].astype(BF))
-    for i in range(count):
-        half_ref[i] = half[i]
-        vec_ref[i] = jnp.concatenate([
-            jnp.sum(input_grad[i], axis=0, keepdims=True),
-            -jnp.sum(decay_cot[i] * softplus(gate[i]), axis=0, keepdims=True)], axis=0)
+    heads = vec_acc.shape[0] // 2
+    even = core_ref[0] == 0
+    span = count // 2 * N
+    at = pl.multiple_of(step * span, N)
+    first, second = (jnp.concatenate(half[a:a + count // 2], axis=0) for a in (0, count // 2))
+    keep_ref[pl.ds(at, span), :] = jnp.where(even, first, second)
+    give_ref[pl.ds(at, span), :] = jnp.where(even, second, first)
+    for i in range(count):
+        vec_acc[pl.ds(base + i, 1), :] = jnp.sum(input_grad[i], axis=0, keepdims=True)
+        vec_acc[pl.ds(heads + base + i, 1), :] = -jnp.sum(
+            decay_cot[i] * soft_ref[i], axis=0, keepdims=True)
     low_acc[...] += sum(each(lambda i: dot(half[i], up[i], 1, 1)))
     score_acc[...] += sum(each(lambda i: jnp.where(
         col == base + i, beta_cot[i] * beta[i] * (1.0 - beta[i]), 0.0)))
 
     @pl.when(step == pl.num_programs(0) - 1)
     def _():
-        lowg_ref[...] = low_acc[...].astype(BF)
-        score_ref[...] = score_acc[...].T[0:score_ref.shape[0], :].astype(BF)
-
-
-def weights_kernel(hid_ref, got_ref, out_ref, *, heads, rows):
-    seqs = got_ref.shape[0]
-    low_at = heads * N
-    score_at = low_at + N
-    down = jnp.zeros((rows, N), F32)
-    beta = jnp.zeros((16, rows), F32)
-    ups = [jnp.zeros((N, N), F32) for _ in range(heads)]
-    vec = jnp.zeros((got_ref.shape[1] - score_at - 16, N), F32)
-    for s in range(seqs):
-        hid = hid_ref[s, 0:rows, :]
-        rank = hid_ref[s, rows:rows + N, :]
-        down = down + dot(hid, got_ref[s, low_at:low_at + N, :])
-        beta = beta + dot(got_ref[s, score_at:score_at + 16, :], hid, 1, 1)
-        for h in range(heads):
-            ups[h] = ups[h] + dot(rank, got_ref[s, h * N:(h + 1) * N, :], 0, 0)
-        vec = vec + got_ref[s, score_at + 16:, :].astype(F32)
-    half = vec.shape[0] // 2
+        low = low_acc[...].astype(BF)
+        score = score_acc[...].T[0:score_ref.shape[0], :].astype(BF)
+        lowg_ref[...] = low
+        score_ref[...] = score
+        common = jnp.concatenate([low, score] + split(vec_acc[...]), axis=0)
+        keep_ref[heads // 2 * N:, :] = common
+        give_ref[heads // 2 * N:, :] = common
+
+
+def terms_kernel(core_ref, hid_ref, hid2_ref, rank_ref, rank2_ref, keep_ref, got_ref, out_ref, *,
+                 own, rows):
+    pairs = out_ref.shape[0]
+    core = core_ref[0]
+    halves = pairs * own * N
+    both = lambda a, b: jnp.concatenate(
+        [keep_ref[halves + a:halves + b, :], got_ref[halves + a:halves + b, :]], axis=0)
+    low = both(0, N)
+    score = jnp.concatenate([keep_ref[halves + N:halves + N + 16, :],
+                             got_ref[halves + N:halves + N + 16, :]], axis=1)
+    at = halves + N + 16
+    vec = keep_ref[at:, :].astype(F32) + got_ref[at:, :].astype(F32)
+    vec = vec[:vec.shape[0] // 2] + vec[vec.shape[0] // 2:]
+    rank = jnp.concatenate([rank_ref[...], rank2_ref[...]], axis=0)
+    for x in range(pairs):
+        start = pl.multiple_of((2 * x + core) * rows, 16)
+        hid = jnp.concatenate([hid_ref[pl.ds(start, rows), :], hid2_ref[pl.ds(start, rows), :]], axis=1)
+        parts = []
+        for h in range(own):
+            a = (x * own + h) * N
+            half = jnp.concatenate([keep_ref[a:a + N, :], got_ref[a:a + N, :]], axis=0)
+            parts.append(dot(rank, half, 0, 0))
+        parts += [dot(hid, low), vec]
+        beta = dot(score, hid, 1, 1)
+        for a in range(0, rows, N):
+            piece = beta[:, a:min(a + N, rows)]
+            if piece.shape[1] < N:
+                piece = jnp.concatenate([piece, jnp.zeros((16, N - piece.shape[1]), F32)], axis=1)
+            parts.append(piece)
+        out_ref[x] = jnp.concatenate(parts, axis=0).astype(out_ref.dtype)
+
+
+def unpack_kernel(sum_ref, down_ref, up_ref, beta_ref, bias_ref, rate_ref):
+    heads, rows = beta_ref.shape
     at = 0
-    for up in ups:
-        out_ref[at:at + N, :] = up
+    for a in range(0, up_ref.shape[1], N):
+        up_ref[:, a:a + N] = sum_ref[at:at + N, :].astype(F32)
         at += N
-    out_ref[at:at + rows, :] = down
+    down_ref[...] = sum_ref[at:at + rows, :].astype(F32)
     at += rows
-    out_ref[at:at + half, :] = vec[:half] + vec[half:]
-    at += half
-    for piece in range(0, rows, N):
-        width = min(N, rows - piece)
-        if width < N:
-            out_ref[at:at + 16, :] = jnp.zeros((16, N), F32)
-        out_ref[at:at + 16, 0:width] = beta[:, piece:piece + width]
-        at += 16
-    out_ref[at:, :] = jnp.zeros((out_ref.shape[0] - at, N), F32)
-
-
-def call(kernel, name, **kw):
+    bias_ref[...] = sum_ref[at:at + heads, :].astype(F32)
+    rate_ref[...] = sum_ref[at + heads:at + 2 * heads, :].astype(F32)
+    at += 2 * heads
+    for a in range(0, rows, N):
+        size = min(N, rows - a)
+        beta_ref[:, a:a + size] = sum_ref[at:at + heads, 0:size].astype(F32)
+        at += heads
+
+
+def call(kernel, name, mib=MIB, **kw):
     return pl.pallas_call(kernel, interpret=INTERPRET, name=name,
-                          compiler_params=pltpu.CompilerParams(vmem_limit_bytes=56 << 20), **kw)
+                          compiler_params=pltpu.CompilerParams(vmem_limit_bytes=mib << 20), **kw)
 
 
 def shape(dims, dtype):
@@ -317,23 +404,27 @@
     inner = heads * N
     rows = width // nf
     own = heads // nf
-    group = heads // nz
+    assert ny == 2 and nz == heads
     hidden_rows = hidden.reshape(tok, width)
 
-    beta_rows = rows * heads // N
     up_rows = own * N
-    mine = jnp.concatenate([
-        gate_up.reshape(N, own, N).swapaxes(0, 1).reshape(up_rows, N),
-        gate_down,
-        beta_weight.reshape(beta_rows, N)], axis=0)
-    mine = jnp.pad(mine, ((0, -mine.shape[0] % 16), (0, 0)))
-    got = lax.all_to_all(jnp.broadcast_to(mine[None], (nf,) + mine.shape), "fsdp", 0, 0, tiled=True)
-    ups = got[:, :up_rows, :].reshape(heads, N, N)
-    down_full = got[:, up_rows:up_rows + rows, :].reshape(width, N)
-    beta_full = got[:, up_rows + rows:up_rows + rows + beta_rows, :].reshape(width, heads)
-
-    low_rank = jnp.dot(hidden_rows, down_full, preferred_element_type=F32).astype(BF)
-    beta_gate = jax.nn.sigmoid(jnp.dot(hidden_rows, beta_full, preferred_element_type=F32))
+    pieces = -(-rows // N)
+    weight_rows = up_rows + rows + pieces * heads
+    turned = hidden_rows.T
+    message = call(pack_kernel, "pack", out_shape=shape((nf // 2, weight_rows, N), BF))(
+        gate_up, gate_down, beta_weight.T)
+    got = lax.all_to_all(message, "x", 0, 0, tiled=True)
+    swapped = lax.ppermute(got, "core", [(0, 1), (1, 0)])
+    core = lax.axis_index("core").astype(jnp.int32).reshape(1)
+    vmem = pl.BlockSpec(memory_space=pltpu.VMEM)
+    ups, down_full, betas, low_rank, beta_gate = call(
+        functools.partial(arrange_kernel, rows=rows), "arrange",
+        in_specs=[pl.BlockSpec(memory_space=pltpu.SMEM)] + [vmem] * 4,
+        out_shape=[shape((heads, N, N), BF), shape((width, N), BF),
+                   shape((nf, pieces * heads, N), BF), shape((tok, N), BF), shape((tok, heads), F32)],
+    )(core, got, swapped, hidden_rows, turned)
+    betas = betas.reshape(nf, pieces, heads, N).transpose(2, 0, 1, 3)
+    betas = betas.reshape(heads, nf, pieces * N)[:, :, :rows].reshape(heads, width)
     bias = gate_bias.reshape(1, inner)
     rate = decay_rate.reshape(1, inner)
     q, k, v, g = (x.reshape(tok, inner) for x in (query_heads, key_heads, value_heads, out_grad))
@@ -351,111 +442,97 @@
 
     hb = FIRST_HB
     send, inv, mix, sco, cum = call(
-        first_kernel, "first",
+        first_kernel, "first", 28,
         grid=(heads // hb,),
         in_specs=gate_specs(hb) + [tok_spec(hb)] * 3,
         out_specs=[pl.BlockSpec((hb, 2 * N, N), lambda i: (i, 0, 0))] + [mat_spec(hb)] * 4,
         out_shape=[shape((heads, 2 * N, N), BF)] + [mat] * 4,
     )(*gate_args, q, k, g)
 
-    spread = lax.all_to_all(send, "z", 0, 0, tiled=True).reshape(nz, group, 2 * N, N)
+    spread = lax.all_to_all(send, "z", 0, 0, tiled=True)
 
     hb = HB
-    q_grad, rest, upd, y, kms, term = call(
-        middle_kernel, "middle",
+    q_grad, rest, upd, y, kms, term, soft, slope = call(
+        middle_kernel, "middle", 56,
         grid=(heads // hb,),
-        in_specs=[whole((tok, heads))] + [tok_spec(hb)] * 4 + [mat_spec(hb)] * 4,
-        out_specs=[tok_spec(hb)] + [mat_spec(hb)] * 5,
-        out_shape=[shape((tok, inner), BF)] + [mat] * 5,
+        in_specs=gate_specs(hb) + [tok_spec(hb)] * 4 + [mat_spec(hb)] * 4,
+        out_specs=[tok_spec(hb)] + [mat_spec(hb)] * 7,
+        out_shape=[shape((tok, inner), BF)] + [mat] * 7,
         cost_estimate=cost,
-    )(beta_gate, q, k, v, g, start, inv, sco, cum)
-
-    every, total = call(
+    )(*gate_args, q, k, v, g, start, inv, sco, cum)
+
+    maps, adds, total = call(
         chain_kernel, "chain",
-        out_shape=[shape((nz, group, N, 2 * N), F32), shape((group, N, 2 * N), BF)],
+        out_shape=[shape((heads, N, N), BF), mat, shape((N, N), BF)],
     )(spread)
-    later = [lax.ppermute(total, "y", [(y + d, y) for y in range(ny - d)])
-             for d in range(ny - 1, 0, -1)]
-    end = call(apply_kernel, "apply", out_shape=shape((nz, group, N, N), BF))(every, *later)
-    end = lax.all_to_all(end.reshape(heads, N, N), "z", 0, 0, tiled=True)
-
-    early = jnp.concatenate([
-        hidden_rows.T.reshape(nf, rows, tok),
-        jnp.broadcast_to(low_rank[None], (nf, tok, N))], axis=1)
-    end, early = lax.optimization_barrier((end, early))
-    early = lax.all_to_all(early, "fsdp", 0, 0, tiled=True)
-
-    k_grad, v_grad, half, vec, low_grad, score = call(
-        second_kernel, "second",
+    later = lax.ppermute(total, "y", [(1, 0)])
+    end = call(apply_kernel, "apply", out_shape=shape((heads, N, N), BF))(maps, adds, later)
+    end = lax.all_to_all(end, "z", 0, 0, tiled=True)
+
+    swap = [(0, 1), (1, 0)]
+    turned2 = lax.ppermute(turned, "core", swap)
+    low_rank2 = lax.ppermute(low_rank, "core", swap)
+
+    assert hb == 2 * own
+    keep_rows = heads // 2 * N + N + heads + 4 * heads
+    k_grad, v_grad, keep, give, low_grad, score = call(
+        second_kernel, "second", 56,
         grid=(heads // hb,),
-        in_specs=gate_specs(hb) + [tok_spec(hb)] + [mat_spec(hb)] * 10,
-        out_specs=[tok_spec(hb)] * 2 + [
-            mat_spec(hb), pl.BlockSpec((hb, 2, N), lambda i: (i, 0, 0)),
-            whole((N, N)), whole((heads, N))],
-        out_shape=[shape((tok, inner), BF)] * 2 + [
-            shape((heads, N, N), BF), shape((heads, 2, N), F32),
+        in_specs=[pl.BlockSpec(memory_space=pltpu.SMEM), mat_spec(hb), whole((tok, heads)), tok_spec(hb)] + [mat_spec(hb)] * 12,
+        out_specs=[tok_spec(hb)] * 2 + [whole((keep_rows, N))] * 2 + [whole((N, N)), whole((heads, N))],
+        out_shape=[shape((tok, inner), BF)] * 2 + [shape((keep_rows, N), BF)] * 2 + [
             shape((N, N), BF), shape((heads, N), BF)],
-        scratch_shapes=[pltpu.VMEM((N, N), F32)] * 2,
+        scratch_shapes=[pltpu.VMEM((N, N), F32)] * 2 + [pltpu.VMEM((2 * heads, N), F32)],
         cost_estimate=cost,
-    )(*gate_args, k, start, end, inv, mix, cum, rest, upd, y, kms, term)
-
-    vec = vec.reshape(2 * heads, N)
-    vec_hi = vec.astype(BF)
-    vec_lo = (vec - vec_hi.astype(F32)).astype(BF)
-    common = jnp.concatenate([low_grad, score, vec_hi, vec_lo], axis=0)
-    terms = jnp.concatenate([
-        half.reshape(nf, own * N, N),
-        jnp.broadcast_to(common[None], (nf,) + common.shape)], axis=1)
-    terms = lax.all_to_all(terms, "fsdp", 0, 0, tiled=True)
-    beta_out = 16 * -(-rows // N)
-    used = own * N + rows + 2 * heads + beta_out
+    )(core, ups, beta_gate, k, start, end, inv, mix, cum, rest, upd, y, kms, term, soft, slope)
+
+    given = lax.ppermute(give, "core", swap)
+    used = own * N + rows + 2 * heads + pieces * heads
+    terms = call(
+        functools.partial(terms_kernel, own=own, rows=rows), "terms",
+        in_specs=[pl.BlockSpec(memory_space=pltpu.SMEM)] + [vmem] * 6,
+        out_shape=shape((nf // 2, used, N), LINK),
+    )(core, turned, turned2, low_rank, low_rank2, keep, given)
+    terms = lax.all_to_all(terms, "x", 0, 0, tiled=True)
     parts = ny * nz
     chunk = 8 * -(-used // (8 * parts))
-    sums = call(
-        functools.partial(weights_kernel, heads=own, rows=rows), "weights",
-        out_shape=shape((parts * chunk, N), F32),
-    )(early, terms)
-    sums = lax.all_to_all(sums.reshape(parts, chunk, N), ("y", "z"), 0, 0, tiled=True)
-    sums = jnp.broadcast_to(jnp.sum(sums, axis=0)[None], (parts, chunk, N))
-    sums = lax.all_to_all(sums, ("y", "z"), 0, 0, tiled=True).reshape(parts * chunk, N)
-    at = own * N
-    up_grad = sums[:at].reshape(own, N, N).swapaxes(0, 1).reshape(N, own * N)
-    down_grad = sums[at:at + rows]
-    at += rows
-    vectors = sums[at:at + 2 * heads].reshape(heads, 2, N).swapaxes(0, 1).reshape(2, inner)
-    at += 2 * heads
-    beta_grad = sums[at:at + beta_out].reshape(-1, 16, N).swapaxes(0, 1).reshape(16, -1)
-    beta_grad = beta_grad[:, :rows].T
+    sums = jnp.sum(terms.astype(F32), axis=0).astype(LINK)
+    sums = jnp.pad(sums, ((0, parts * chunk - used), (0, 0))).reshape(parts, chunk, N)
+    sums = lax.all_to_all(sums, ("y", "z"), 0, 0, tiled=True)
+    sums = jnp.sum(sums.astype(F32), axis=0).astype(LINK)
+    sums = lax.all_to_all(jnp.broadcast_to(sums[None], (parts, chunk, N)), ("y", "z"), 0, 0, tiled=True)
+    down_grad, up_grad, beta_grad, bias_grad, rate_grad = call(
+        unpack_kernel, "unpack",
+        out_shape=[shape((rows, N), F32), shape((N, own * N), F32), shape((heads, rows), F32),
+                   shape((heads, N), F32), shape((heads, N), F32)],
+    )(sums.reshape(parts * chunk, N))
 
     hidden_grad = (
         lax.dot_general(low_grad, down_full, (((1,), (1,)), ((), ())), preferred_element_type=F32)
-        + lax.dot_general(score, beta_full, (((0,), (1,)), ((), ())), preferred_element_type=F32)
+        + lax.dot_general(score, betas, (((0,), (0,)), ((), ())), preferred_element_type=F32)
     ).astype(BF)
 
     return (q_grad[None], k_grad[None], v_grad[None], hidden_grad[None],
-            down_grad, up_grad, beta_grad, vectors[0], vectors[1])
-
-
-def grid_of(size):
-    ny = 1
-    while ny * ny * 4 <= size:
-        ny *= 2
-    return ny, size // ny
+            down_grad, up_grad, beta_grad.T, bias_grad.reshape(inner), rate_grad.reshape(inner))
+
+
+def grid_of(size, heads=16):
+    return size // heads, heads
 
 
 def solution(mesh):
     nf, size = mesh.shape["fsdp"], mesh.shape["ctx"]
     ny, nz = grid_of(size)
-    fine = Mesh(mesh.devices.reshape(nf, ny, nz), ("fsdp", "y", "z"))
-    ctx = ("y", "z")
-    tokens = P("fsdp", ctx, None)
+    fine = Mesh(mesh.devices.reshape(nf // 2, 2, ny, nz), ("x", "core", "y", "z"))
+    fsdp, ctx = ("x", "core"), ("y", "z")
+    tokens = P(fsdp, ctx, None)
     return jax.shard_map(
         functools.partial(on_device, nf, ny, nz),
         mesh=fine,
         in_specs=(tokens,) * 5 + (
-            P("fsdp", ctx, None, None, None), P("fsdp", None), P(None, "fsdp"), P(), P(),
-            P("fsdp", None)),
+            P(fsdp, ctx, None, None, None), P(fsdp, None), P(None, fsdp), P(), P(),
+            P(fsdp, None)),
         out_specs=(tokens,) * 4 + (
-            P("fsdp", None), P(None, "fsdp"), P("fsdp", None), P(), P()),
+            P(fsdp, None), P(None, fsdp), P(fsdp, None), P(), P()),
         check_vma=False,
     )

time: 199 us -> 157 us (0.79)
  blocking collectives: 96.4 us -> 64.5 us
  Pallas kernels: 38.3 us -> 31.5 us
  waiting for transfers between devices: 28.4 us -> 33.4 us
  other arithmetic: 4.58 us -> 0.16 us
    all_to_all x4 -> x3, blocking collectives: 96.4 us -> 64.5 us  [the longest x1 36.2 us: on_device(): spread = lax.all_to_all(send, 'z', 0, 0, tiled=True)]
    pallas_call x6 -> x9, Pallas kernels: 38.3 us -> 31.5 us  [the longest x1 10.1 us: on_device(): call(second_kernel, 'second', 56, grid=(heads // hb,), in_specs=[pl.Block...]
    all_to_all x3, waiting for transfers between devices: 19.4 us -> 24.3 us  [the longest x1 10.2 us: on_device(): sums = lax.all_to_all(sums, ('y', 'z'), 0, 0, tiled=True)]
    unnamed x18 -> x47, local copies, waits for them, and re-layouts: 2.17 us -> 6.26 us
    concatenate x4 -> x0, other arithmetic: 3.74 us -> none  [the longest x1 1.11 us: on_device(): jnp.concatenate([half.reshape(nf, own * N, N), jnp.broadcast_to(common[No...]
    dot_general x3 -> x1, matrix products: 3.04 us -> 0.34 us  [on_device(): lax.dot_general(score, betas, (((0,), (0,)), ((), ())), preferred_element...]
    slice x8 -> x0, local copies, waits for them, and re-layouts: 2.17 us -> none  [the longest x1 0.83 us: on_device(): ups = got[:, :up_rows, :].reshape(heads, N, N)]
    ppermute x3 -> x5, waiting for transfers between devices: 9.06 us -> 9.08 us  [the longest x1 6.01 us: on_device(): later = lax.ppermute(total, 'y', [(1, 0)])]
  transfers between devices with their start and end apart: 6 -> 8, of which waited for: 6 -> 6; matrix products, arithmetic and copies ran while one was open for 3% -> 1% of each run, Pallas kernels for 9% -> 12%
where the time goes in v2:
time: 157 us; the launch traced here: 156 us
  blocking collectives  64.5 us (41%)
  waiting for transfers between devices  33.4 us (21%)
  Pallas kernels  31.5 us (20%)
  starting transfers between devices  16.7 us (11%)
  local copies, waits for them, and re-layouts  7.81 us (5%)
    all_to_all x1, blocking collectives, on_device(): spread = lax.all_to_all(send, 'z', 0, 0, tiled=True)  36.2 us
    all_to_all x1, blocking collectives, on_device(): got = lax.all_to_all(message, 'x', 0, 0, tiled=True)  14.4 us
    all_to_all x1, blocking collectives, on_device(): terms = lax.all_to_all(terms, 'x', 0, 0, tiled=True)  13.8 us
    all_to_all x1, waiting for transfers between devices, on_device(): sums = lax.all_to_all(sums, ('y', 'z'), 0, 0, tiled=True)  10.2 us
    pallas_call x1, Pallas kernels, on_device(): call(second_kernel, 'second', 56, grid=(heads // hb,), in_specs=[pl.Block...  10.1 us
    all_to_all x1, waiting for transfers between devices, on_device(): lax.all_to_all(jnp.broadcast_to(sums[None], (parts, chunk, N)), ('y', 'z'...  8.99 us
    pallas_call x1, Pallas kernels, on_device(): call(middle_kernel, 'middle', 56, grid=(heads // hb,), in_specs=gate_spec...  8.77 us
    pallas_call x1, Pallas kernels, on_device(): call(first_kernel, 'first', 28, grid=(heads // hb,), in_specs=gate_specs(...  7.9 us
  transfers between devices with their start and end apart: 8, of which 6 were waited for; matrix products, arithmetic and copies ran while one was open for 1% of the time, Pallas kernels for 12%

profile of v2, /device:TPU:32, one launch (start us, length us, event | category | flops | bytes accessed | tf_op | source)
XLA Modules:
  0.0 156.5 jit_solution(12976587550973651054)
XLA Ops:
  0.6 0.0 copy-start
  0.7 0.0 copy-start.10
  0.7 0.9 copy-done.10
  1.6 0.8 copy-done.11
  2.4 0.7 copy-done.13
  3.1 0.1 pack.1
  3.2 14.4 %all_to_all.30.ours_ref = bf16[4,592,128]{2,1,0:T(8,128)(2,1)S(1)} all-to-all(bf16[4,592,128]{2,1,0:T(8,128)(2,1)S(1)} %pack.1), channel_id=1, replica_groups=mesh['x'=4,'core'=2,'y'=2,'z'=16] {'x'}, dimensions={0} | all-to-all | bytes 1212416 | tf_op jit(solution)/shard_map/all_to_all | solution.py:416
  17.7 0.0 collective-permute-start
  17.7 0.0 copy-done
  17.7 0.3 copy.25
  18.0 1.7 %collective-permute-done.theirs_ref = bf16[4,592,128]{2,1,0:T(8,128)(2,1)S(1)} collective-permute-done((bf16[4,592,128]{2,1,0:T(8,128)(2,1)S(1)}, bf16[4,592,128]{2,1,0:T(8,128)(2,1)S(1)}, u32[]{:S(2)}, u32[]{:S(2)}) %collective-permute-start) | collective-permute-done | bytes 606240 | tf_op jit(solution)/shard_map/ppermute | solution.py:417
  19.7 0.0 copy-start.15
  19.7 0.6 arrange.1
  20.4 0.0 copy-start.8
  20.4 0.0 copy-start.12
  20.4 0.0 copy-start.4
  20.4 0.0 copy-start.6
  20.4 0.3 copy-done.1
  20.7 0.2 copy-done.2
  20.9 0.2 copy-done.3
  21.1 0.0 copy-done.14
  21.1 0.0 copy-done.15
  21.1 7.9 %first.1 = (bf16[16,256,128]{2,1,0:T(8,128)(2,1)S(1)}, f32[16,128,128]{2,1,0:T(8,128)S(1)}, f32[16,128,128]{2,1,0:T(8,128)S(1)}, f32[16,128,128]{2,1,0:T(8,128)S(1)}, f32[16,128,128]{2,1,0:T(8,128)S(1)}) custom-call(bf16[128,128]{1,0:T(8,128)(2,1)S(1)} %get-tuple-element.41.low_ref.rank_ref, bf16[16,128,128]{2,1,0:T(8,128)(2,1)S(1)} %get-tuple-element.42.up_ref, ...), custom_call_target="tpu_custom_call" | custom-call | tf_op jit(solution)/shard_map/first/pallas_call | solution.py:444
  29.0 0.0 copy-done.8
  29.0 0.0 copy-done.12
  29.0 0.0 copy-start.16
  29.0 1.0 copy-done.16
  30.0 36.2 %all_to_all.31.got_ref = bf16[16,256,128]{2,1,0:T(8,128)(2,1)S(1)} all-to-all(bf16[16,256,128]{2,1,0:T(8,128)(2,1)S(1)} %get-tuple-element.48), channel_id=1, replica_groups=mesh['x'=4,'core'=2,'y'=2,'z'=16] {'z'}, dimensions={0} | all-to-all | bytes 2097152 | tf_op jit(solution)/shard_map/all_to_all | solution.py:452
  66.2 0.0 copy-done.4
  66.2 0.0 copy-done.6
  66.2 1.6 %chain.1 = (bf16[16,128,128]{2,1,0:T(8,128)(2,1)S(1)}, f32[16,128,128]{2,1,0:T(8,128)S(1)}, bf16[128,128]{1,0:T(8,128)(2,1)S(1)}) custom-call(bf16[16,256,128]{2,1,0:T(8,128)(2,1)S(1)} %all_to_all.31.got_ref), custom_call_target="tpu_custom_call" | custom-call | tf_op jit(solution)/shard_map/chain/pallas_call | solution.py:464
  67.9 0.0 copy-done.17
  67.9 0.0 copy-done.18
  67.9 0.0 copy-done.19
  67.9 1.3 collective-permute-start.1
  69.2 6.0 %collective-permute-done.1.later_ref = bf16[128,128]{1,0:T(8,128)(2,1)S(1)} collective-permute-done((bf16[128,128]{1,0:T(8,128)(2,1)S(1)}, bf16[128,128]{1,0:T(8,128)(2,1)S(1)}, u32[]{:S(2)}, u32[]{:S(2)}) %collective-permute-start.1) | collective-permute-done | bytes 32800 | tf_op jit(solution)/shard_map/ppermute | solution.py:468
  75.2 1.1 apply.1
  76.3 4.9 %all-to-all-start.2 = ((bf16[16,128,128]{2,1,0:T(8,128)(2,1)}), bf16[16,128,128]{2,1,0:T(8,128)(2,1)S(1)}, u32[]{:S(2)}, u32[]{:S(2)}) async-start(bf16[16,128,128]{2,1,0:T(8,128)(2,1)} %apply.1), calls=%async_computation.2 | async-start | bytes 1048576 | tf_op jit(solution)/shard_map/all_to_all | solution.py:470
  81.2 0.0 collective-permute-start.2
  81.2 8.8 %middle.1 = (bf16[128,2048]{1,0:T(8,128)(2,1)}, f32[16,128,128]{2,1,0:T(8,128)}, f32[16,128,128]{2,1,0:T(8,128)}, f32[16,128,128]{2,1,0:T(8,128)}, f32[16,128,12...) custom-call(bf16[128,128]{1,0:T(8,128)(2,1)} %copy-done.6, ...), custom_call_target="tpu_custom_call" | custom-call | flops 4000000000 | bytes 12582912 | tf_op jit(solution)/shard_map/middle/pallas_call | solution.py:455
  90.0 5.1 %all-to-all-done.2.end_ref = bf16[16,128,128]{2,1,0:T(8,128)(2,1)S(1)} async-done(((bf16[16,128,128]{2,1,0:T(8,128)(2,1)}), bf16[16,128,128]{2,1,0:T(8,128)(2,1)S(1)}, u32[]{:S(2)}, u32[]{:S(2)}) %all-to-all-start.2) | async-done | bytes 524320 | tf_op jit(solution)/shard_map/all_to_all | solution.py:470
  95.1 0.8 copy-done.20
  95.9 10.1 %second.1 = (bf16[128,2048]{1,0:T(8,128)(2,1)}, bf16[128,2048]{1,0:T(8,128)(2,1)}, bf16[1232,128]{1,0:T(8,128)(2,1)}, bf16[1232,128]{1,0:T(8,128)(2,1)}, bf16[12...) custom-call(s32[1]{0:T(128)} %bitcast.core_ref, bf16[16,128,128]{2,1,0:T(8,128)(2,1)} %copy-done.4, f32[128,16]{1,0:T(8,128)} %copy-done.12, ...), custom_call_target="tpu_custom_call" | custom-call | flops 4000000000 | bytes 12582912 | tf_op jit(solution)/shard_map/second/pallas_call | solution.py:478
  106.0 0.1 collective-permute-start.4
  106.1 0.5 collective-permute-start.3
  106.6 0.0 collective-permute-done.2.hid2_ref
  106.6 1.4 collective-permute-done.3.rank2_ref
  108.0 0.0 collective-permute-done.4.got_ref
  108.0 1.0 copy-done.5
  108.9 0.6 terms.1
  109.5 0.0 copy-start.9
  109.5 13.8 %all_to_all.32 = bf16[4,624,128]{2,1,0:T(8,128)(2,1)S(1)} all-to-all(bf16[4,624,128]{2,1,0:T(8,128)(2,1)S(1)} %terms.1), channel_id=1, replica_groups=mesh['x'=4,'core'=2,'y'=2,'z'=16] {'x'}, dimensions={0} | all-to-all | bytes 1277952 | tf_op jit(solution)/shard_map/all_to_all | solution.py:496
  123.4 0.1 reduce_sum.24
  123.5 0.7 pad.4
  124.2 5.4 %all-to-all-start.4 = ((bf16[32,24,128]{2,1,0:T(8,128)(2,1)}), bf16[32,24,128]{2,1,0:T(8,128)(2,1)S(1)}, u32[]{:S(2)}, u32[]{:S(2)}) async-start(bf16[32,24,128]{2,1,0:T(8,128)(2,1)} %bitcast.20), calls=%async_computation.4 | async-start | bytes 393216 | tf_op jit(solution)/shard_map/all_to_all | solution.py:501
  129.7 0.1 reshape.78
  129.8 10.2 %all-to-all-done.4 = bf16[32,24,128]{2,1,0:T(8,128)(2,1)S(1)} async-done(((bf16[32,24,128]{2,1,0:T(8,128)(2,1)}), bf16[32,24,128]{2,1,0:T(8,128)(2,1)S(1)}, u32[]{:S(2)}, u32[]{:S(2)}) %all-to-all-start.4) | async-done | bytes 196640 | tf_op jit(solution)/shard_map/all_to_all | solution.py:501
  140.1 0.7 broadcast_in_dim.22
  140.8 4.5 %all-to-all-start.5 = ((bf16[32,24,128]{2,1,0:T(8,128)(2,1)}), bf16[32,24,128]{2,1,0:T(8,128)(2,1)S(1)}, u32[]{:S(2)}, u32[]{:S(2)}) async-start(bf16[32,24,128]{2,1,0:T(8,128)(2,1)} %broadcast_in_dim.22), calls=%async_computation.5 | async-start | bytes 393216 | tf_op jit(solution)/shard_map/all_to_all | solution.py:503
  145.3 0.3 fusion.2
  145.6 0.0 copy-done.21
  145.6 1.1 fusion.1
  146.8 9.0 %all-to-all-done.5 = bf16[32,24,128]{2,1,0:T(8,128)(2,1)S(1)} async-done(((bf16[32,24,128]{2,1,0:T(8,128)(2,1)}), bf16[32,24,128]{2,1,0:T(8,128)(2,1)S(1)}, u32[]{:S(2)}, u32[]{:S(2)}) %all-to-all-start.5) | async-done | bytes 196640 | tf_op jit(solution)/shard_map/all_to_all | solution.py:503
  155.8 0.7 unpack.1
  (19 shorter events, 0.1 us)
Async XLA Ops:
  0.6 17.0 %copy-start = (bf16[1,128,2304]{2,1,0:T(8,128)(2,1)S(1)}, bf16[1,128,2304]{2,1,0:T(8,128)(2,1)}, u32[]{:S(2)}) copy-start(bf16[1,128,2304]{2,1,0:T(8,128)(2,1)} %param.11) | copy-start | bytes 1769476
  0.7 0.9 copy-start.10
  1.6 0.8 copy-start.11
  2.4 0.7 copy-start.13
  17.7 2.0 %collective-permute-start = (bf16[4,592,128]{2,1,0:T(8,128)(2,1)S(1)}, bf16[4,592,128]{2,1,0:T(8,128)(2,1)S(1)}, u32[]{:S(2)}, u32[]{:S(2)}) collective-permute-start(bf16[4,592,128]{2,1,0:T(8,128)(2,1)S(1)} %all_to_all.30.ours_ref), channel_id=1, source_target_pairs={{0,32},{32,0},{1,33},{33,1},{2,34},{34,2},{3,35},{35,3},{4,36},{36... | collective-permute-start | bytes 1818632 | tf_op jit(solution)/shard_map/ppermute | solution.py:417
  19.7 1.0 copy-start.1
  19.7 1.2 copy-start.2
  19.7 1.4 copy-start.3
  19.7 1.4 copy-start.14
  19.7 1.4 copy-start.15
  20.4 8.6 %copy-start.8 = (bf16[8,48,128]{2,1,0:T(8,128)(2,1)}, bf16[8,48,128]{2,1,0:T(8,128)(2,1)S(1)}, u32[]{:S(2)}) copy-start(bf16[8,48,128]{2,1,0:T(8,128)(2,1)S(1)} %get-tuple-element.65) | copy-start | bytes 294916
  20.4 8.6 %copy-start.12 = (f32[128,16]{1,0:T(8,128)}, f32[128,16]{1,0:T(8,128)S(1)}, u32[]{:S(2)}) copy-start(f32[128,16]{1,0:T(8,128)S(1)} %get-tuple-element.43.beta_ref) | copy-start | bytes 24580
  20.4 45.8 %copy-start.4 = (bf16[16,128,128]{2,1,0:T(8,128)(2,1)}, bf16[16,128,128]{2,1,0:T(8,128)(2,1)S(1)}, u32[]{:S(2)}) copy-start(bf16[16,128,128]{2,1,0:T(8,128)(2,1)S(1)} %get-tuple-element.42.up_ref) | copy-start | bytes 1572868
  20.4 45.8 %copy-start.6 = (bf16[128,128]{1,0:T(8,128)(2,1)}, bf16[128,128]{1,0:T(8,128)(2,1)S(1)}, u32[]{:S(2)}) copy-start(bf16[128,128]{1,0:T(8,128)(2,1)S(1)} %get-tuple-element.41.low_ref.rank_ref) | copy-start | bytes 98308
  29.0 1.0 copy-start.16
  30.0 37.9 %copy-start.17 = (f32[16,128,128]{2,1,0:T(8,128)}, f32[16,128,128]{2,1,0:T(8,128)S(1)}, u32[]{:S(2)}) copy-start(f32[16,128,128]{2,1,0:T(8,128)S(1)} %get-tuple-element.52.mix_ref) | copy-start | bytes 3145732
  30.0 37.9 %copy-start.18 = (f32[16,128,128]{2,1,0:T(8,128)}, f32[16,128,128]{2,1,0:T(8,128)S(1)}, u32[]{:S(2)}) copy-start(f32[16,128,128]{2,1,0:T(8,128)S(1)} %get-tuple-element.46.cum_ref) | copy-start | bytes 3145732
  30.0 37.9 %copy-start.19 = (f32[16,128,128]{2,1,0:T(8,128)}, f32[16,128,128]{2,1,0:T(8,128)S(1)}, u32[]{:S(2)}) copy-start(f32[16,128,128]{2,1,0:T(8,128)S(1)} %get-tuple-element.45.sco_ref) | copy-start | bytes 3145732
  67.9 7.3 %collective-permute-start.1 = (bf16[128,128]{1,0:T(8,128)(2,1)S(1)}, bf16[128,128]{1,0:T(8,128)(2,1)S(1)}, u32[]{:S(2)}, u32[]{:S(2)}) collective-permute-start(bf16[128,128]{1,0:T(8,128)(2,1)S(1)} %get-tuple-element.51), channel_id=1, source_target_pairs={{16,0},{17,1},{18,2},{19,3},{20,4},{21,5},{22,6},{23,7},{24,8},{25... | collective-permute-start | bytes 98312 | tf_op jit(solution)/shard_map/ppermute | solution.py:468
  76.3 18.8 %all-to-all-start.2 = ((bf16[16,128,128]{2,1,0:T(8,128)(2,1)}), bf16[16,128,128]{2,1,0:T(8,128)(2,1)S(1)}, u32[]{:S(2)}, u32[]{:S(2)}) async-start(bf16[16,128,128]{2,1,0:T(8,128)(2,1)} %apply.1), calls=%async_computation.2 | async-start | bytes 1048576 | tf_op jit(solution)/shard_map/all_to_all | solution.py:470
  81.2 25.4 %collective-permute-start.2 = (bf16[2304,128]{1,0:T(8,128)(2,1)S(1)}, bf16[2304,128]{1,0:T(8,128)(2,1)S(1)}, u32[]{:S(2)}, u32[]{:S(2)}) collective-permute-start(bf16[2304,128]{1,0:T(8,128)(2,1)S(1)} %bitcast.35), channel_id=1, source_target_pairs={{0,32},{32,0},{1,33},{33,1},{2,34},{34,2},{3,35},{35,3},{4,36},{36... | collective-permute-start | bytes 1769480 | tf_op jit(solution)/shard_map/ppermute | solution.py:473
  95.1 0.8 copy-start.20
  95.9 10.2 %copy-start.7 = (bf16[128,128]{1,0:T(8,128)(2,1)S(1)}, bf16[128,128]{1,0:T(8,128)(2,1)}, u32[]{:S(2)}) copy-start(bf16[128,128]{1,0:T(8,128)(2,1)} %copy-done.6) | copy-start | bytes 98308
  106.0 2.0 %collective-permute-start.4 = (bf16[1232,128]{1,0:T(8,128)(2,1)}, bf16[1232,128]{1,0:T(8,128)(2,1)S(1)}, u32[]{:S(2)}, u32[]{:S(2)}) collective-permute-start(bf16[1232,128]{1,0:T(8,128)(2,1)} %get-tuple-element.67), channel_id=1, source_target_pairs={{0,32},{32,0},{1,33},{33,1},{2,34},{34,2},{3,35},{35,3},{4,36},{36... | collective-permute-start | bytes 946184 | tf_op jit(solution)/shard_map/ppermute | solution.py:489
  106.1 1.8 %collective-permute-start.3 = (bf16[128,128]{1,0:T(8,128)(2,1)S(1)}, bf16[128,128]{1,0:T(8,128)(2,1)S(1)}, u32[]{:S(2)}, u32[]{:S(2)}) collective-permute-start(bf16[128,128]{1,0:T(8,128)(2,1)S(1)} %copy-done.7), channel_id=1, source_target_pairs={{0,32},{32,0},{1,33},{33,1},{2,34},{34,2},{3,35},{35,3},{4,36},{36... | collective-permute-start | bytes 98312 | tf_op jit(solution)/shard_map/ppermute | solution.py:474
  108.0 1.0 copy-start.5
  109.5 20.1 %copy-start.9 = (bf16[8,48,128]{2,1,0:T(8,128)(2,1)S(1)}, bf16[8,48,128]{2,1,0:T(8,128)(2,1)}, u32[]{:S(2)}) copy-start(bf16[8,48,128]{2,1,0:T(8,128)(2,1)} %copy-done.8) | copy-start | bytes 294916
  123.4 21.9 %copy-start.22 = (bf16[16,128]{1,0:T(8,128)(2,1)S(1)}, bf16[16,128]{1,0:T(8,128)(2,1)}, u32[]{:S(2)}) copy-start(bf16[16,128]{1,0:T(8,128)(2,1)} %get-tuple-element.64) | copy-start | bytes 12292
  124.2 15.8 %all-to-all-start.4 = ((bf16[32,24,128]{2,1,0:T(8,128)(2,1)}), bf16[32,24,128]{2,1,0:T(8,128)(2,1)S(1)}, u32[]{:S(2)}, u32[]{:S(2)}) async-start(bf16[32,24,128]{2,1,0:T(8,128)(2,1)} %bitcast.20), calls=%async_computation.4 | async-start | bytes 393216 | tf_op jit(solution)/shard_map/all_to_all | solution.py:501
  129.6 16.0 %copy-start.21 = (bf16[128,128]{1,0:T(8,128)(2,1)S(1)}, bf16[128,128]{1,0:T(8,128)(2,1)}, u32[]{:S(2)}) copy-start(bf16[128,128]{1,0:T(8,128)(2,1)} %get-tuple-element.62) | copy-start | bytes 98308
  140.8 15.0 %all-to-all-start.5 = ((bf16[32,24,128]{2,1,0:T(8,128)(2,1)}), bf16[32,24,128]{2,1,0:T(8,128)(2,1)S(1)}, u32[]{:S(2)}, u32[]{:S(2)}) async-start(bf16[32,24,128]{2,1,0:T(8,128)(2,1)} %broadcast_in_dim.22), calls=%async_computation.5 | async-start | bytes 393216 | tf_op jit(solution)/shard_map/all_to_all | solution.py:503

commit v3 on v2

--- a/solution.py
+++ b/solution.py
@@ -12,7 +12,7 @@
 F32 = jnp.float32
 N = 128
 HB = 4
-FIRST_HB = 8
+FIRST_HB = 16
 LINK = jnp.bfloat16
 RUN = 4
 MIB = 28
@@ -371,6 +371,22 @@
         out_ref[x] = jnp.concatenate(parts, axis=0).astype(out_ref.dtype)
 
 
+def total(ref):
+    return sum(ref[r].astype(F32) for r in range(ref.shape[0]))
+
+
+def total_kernel(in_ref, out_ref):
+    rows = in_ref.shape[1]
+    out_ref[0:rows, :] = total(in_ref).astype(out_ref.dtype)
+    out_ref[rows:, :] = jnp.zeros((out_ref.shape[0] - rows, N), out_ref.dtype)
+
+
+def share_kernel(in_ref, out_ref):
+    mine = total(in_ref).astype(out_ref.dtype)
+    for r in range(out_ref.shape[0]):
+        out_ref[r] = mine
+
+
 def unpack_kernel(sum_ref, down_ref, up_ref, beta_ref, bias_ref, rate_ref):
     heads, rows = beta_ref.shape
     at = 0
@@ -411,7 +427,7 @@
     pieces = -(-rows // N)
     weight_rows = up_rows + rows + pieces * heads
     turned = hidden_rows.T
-    message = call(pack_kernel, "pack", out_shape=shape((nf // 2, weight_rows, N), BF))(
+    message = call(pack_kernel, "pack", 56, out_shape=shape((nf // 2, weight_rows, N), BF))(
         gate_up, gate_down, beta_weight.T)
     got = lax.all_to_all(message, "x", 0, 0, tiled=True)
     swapped = lax.ppermute(got, "core", [(0, 1), (1, 0)])
@@ -496,11 +512,10 @@
     terms = lax.all_to_all(terms, "x", 0, 0, tiled=True)
     parts = ny * nz
     chunk = 8 * -(-used // (8 * parts))
-    sums = jnp.sum(terms.astype(F32), axis=0).astype(LINK)
-    sums = jnp.pad(sums, ((0, parts * chunk - used), (0, 0))).reshape(parts, chunk, N)
+    sums = call(total_kernel, "total", out_shape=shape((parts * chunk, N), LINK))(terms)
+    sums = lax.all_to_all(sums.reshape(parts, chunk, N), ("y", "z"), 0, 0, tiled=True)
+    sums = call(share_kernel, "share", out_shape=shape((parts, chunk, N), LINK))(sums)
     sums = lax.all_to_all(sums, ("y", "z"), 0, 0, tiled=True)
-    sums = jnp.sum(sums.astype(F32), axis=0).astype(LINK)
-    sums = lax.all_to_all(jnp.broadcast_to(sums[None], (parts, chunk, N)), ("y", "z"), 0, 0, tiled=True)
     down_grad, up_grad, beta_grad, bias_grad, rate_grad = call(
         unpack_kernel, "unpack",
         out_shape=[shape((rows, N), F32), shape((N, own * N), F32), shape((heads, rows), F32),

time: 157 us -> 156 us (level)
  local copies, waits for them, and re-layouts: 7.81 us -> 3.91 us
  Pallas kernels: 31.5 us -> 34.3 us
    pallas_call x1 -> x3, Pallas kernels: 0.08 us -> 3.32 us  [the longest x1 1.84 us: on_device(): call(pack_kernel, 'pack', 56, out_shape=shape((nf // 2, weight_rows, N),...]
    unnamed x47 -> x41, local copies, waits for them, and re-layouts: 6.26 us -> 3.76 us
where the time goes in v3:
time: 156 us; the launch traced here: 155 us
  blocking collectives  64.7 us (41%)
  Pallas kernels  34.3 us (22%)
  waiting for transfers between devices  33.4 us (21%)
  starting transfers between devices  16.7 us (11%)
  local copies, waits for them, and re-layouts  3.91 us (3%)
    all_to_all x1, blocking collectives, on_device(): spread = lax.all_to_all(send, 'z', 0, 0, tiled=True)  36.3 us
    all_to_all x1, blocking collectives, on_device(): got = lax.all_to_all(message, 'x', 0, 0, tiled=True)  14.6 us
    all_to_all x1, blocking collectives, on_device(): terms = lax.all_to_all(terms, 'x', 0, 0, tiled=True)  13.8 us
    all_to_all x1, waiting for transfers between devices, on_device(): lax.all_to_all(sums.reshape(parts, chunk, N), ('y', 'z'), 0, 0, tiled=True)  10.2 us
    pallas_call x1, Pallas kernels, on_device(): call(second_kernel, 'second', 56, grid=(heads // hb,), in_specs=[pl.Block...  10.1 us
    all_to_all x1, waiting for transfers between devices, on_device(): sums = lax.all_to_all(sums, ('y', 'z'), 0, 0, tiled=True)  9 us
    pallas_call x1, Pallas kernels, on_device(): call(middle_kernel, 'middle', 56, grid=(heads // hb,), in_specs=gate_spec...  8.77 us
    pallas_call x1, Pallas kernels, on_device(): call(first_kernel, 'first', 28, grid=(heads // hb,), in_specs=gate_specs(...  7.44 us
  transfers between devices with their start and end apart: 8, of which 6 were waited for; matrix products, arithmetic and copies ran while one was open for 1% of the time, Pallas kernels for 12%

profile of v3, /device:TPU:32, one launch (start us, length us, event | category | flops | bytes accessed | tf_op | source)
XLA Modules:
  0.0 155.4 jit_solution(8268077684648873935)
XLA Ops:
  0.6 0.0 copy-start
  0.7 1.8 %pack.1 = bf16[4,592,128]{2,1,0:T(8,128)(2,1)} custom-call(bf16[128,256]{1,0:T(8,128)(2,1)} %up_ref.1, bf16[288,128]{1,0:T(8,128)(2,1)} %down_ref.1, bf16[16,288]{1,0:T(8,128)(2,1)} %bitcast.52), custom_call_target="tpu_custom_call" | custom-call | tf_op jit(solution)/shard_map/pack/pallas_call | solution.py:430
  2.5 14.6 %all_to_all.30.ours_ref = bf16[4,592,128]{2,1,0:T(8,128)(2,1)S(1)} all-to-all(bf16[4,592,128]{2,1,0:T(8,128)(2,1)} %pack.1), channel_id=1, replica_groups=mesh['x'=4,'core'=2,'y'=2,'z'=16] {'x'}, dimensions={0} | all-to-all | bytes 1212416 | tf_op jit(solution)/shard_map/all_to_all | solution.py:432
  17.1 0.0 collective-permute-start
  17.1 0.0 copy-done
  17.1 0.3 copy.22
  17.5 1.7 %collective-permute-done.theirs_ref = bf16[4,592,128]{2,1,0:T(8,128)(2,1)S(1)} collective-permute-done((bf16[4,592,128]{2,1,0:T(8,128)(2,1)S(1)}, bf16[4,592,128]{2,1,0:T(8,128)(2,1)S(1)}, u32[]{:S(2)}, u32[]{:S(2)}) %collective-permute-start) | collective-permute-done | bytes 606240 | tf_op jit(solution)/shard_map/ppermute | solution.py:433
  19.2 0.0 copy-start.1
  19.2 0.0 copy-start.12
  19.2 0.6 arrange.1
  19.8 0.0 copy-start.8
  19.8 0.0 copy-start.10
  19.9 0.0 copy-start.4
  19.9 0.0 copy-start.6
  19.9 0.3 copy-done.1
  20.2 0.2 copy-done.2
  20.4 0.2 copy-done.3
  20.5 0.0 copy-done.11
  20.5 0.0 copy-done.12
  20.5 7.4 %first.1 = (bf16[16,256,128]{2,1,0:T(8,128)(2,1)S(1)}, f32[16,128,128]{2,1,0:T(8,128)S(1)}, f32[16,128,128]{2,1,0:T(8,128)S(1)}, f32[16,128,128]{2,1,0:T(8,128)S(1)}, f32[16,128,128]{2,1,0:T(8,128)S(1)}) custom-call(bf16[128,128]{1,0:T(8,128)(2,1)S(1)} %get-tuple-element.41.low_ref.rank_ref, bf16[16,128,128]{2,1,0:T(8,128)(2,1)S(1)} %get-tuple-element.42.up_ref, ...), custom_call_target="tpu_custom_call" | custom-call | tf_op jit(solution)/shard_map/first/pallas_call | solution.py:460
  28.0 0.0 copy-done.8
  28.0 0.0 copy-done.10
  28.0 0.0 copy-start.13
  28.0 1.0 copy-done.13
  29.0 36.3 %all_to_all.31.got_ref = bf16[16,256,128]{2,1,0:T(8,128)(2,1)S(1)} all-to-all(bf16[16,256,128]{2,1,0:T(8,128)(2,1)S(1)} %get-tuple-element.48), channel_id=1, replica_groups=mesh['x'=4,'core'=2,'y'=2,'z'=16] {'z'}, dimensions={0} | all-to-all | bytes 2097152 | tf_op jit(solution)/shard_map/all_to_all | solution.py:468
  65.2 0.0 copy-done.4
  65.2 0.0 copy-done.6
  65.2 1.6 %chain.1 = (bf16[16,128,128]{2,1,0:T(8,128)(2,1)S(1)}, f32[16,128,128]{2,1,0:T(8,128)S(1)}, bf16[128,128]{1,0:T(8,128)(2,1)S(1)}) custom-call(bf16[16,256,128]{2,1,0:T(8,128)(2,1)S(1)} %all_to_all.31.got_ref), custom_call_target="tpu_custom_call" | custom-call | tf_op jit(solution)/shard_map/chain/pallas_call | solution.py:480
  66.9 0.0 copy-done.14
  66.9 0.0 copy-done.15
  66.9 0.0 copy-done.16
  66.9 1.3 collective-permute-start.1
  68.2 6.0 %collective-permute-done.1.later_ref = bf16[128,128]{1,0:T(8,128)(2,1)S(1)} collective-permute-done((bf16[128,128]{1,0:T(8,128)(2,1)S(1)}, bf16[128,128]{1,0:T(8,128)(2,1)S(1)}, u32[]{:S(2)}, u32[]{:S(2)}) %collective-permute-start.1) | collective-permute-done | bytes 32800 | tf_op jit(solution)/shard_map/ppermute | solution.py:484
  74.2 1.1 apply.1
  75.3 4.9 %all-to-all-start.2 = ((bf16[16,128,128]{2,1,0:T(8,128)(2,1)}), bf16[16,128,128]{2,1,0:T(8,128)(2,1)S(1)}, u32[]{:S(2)}, u32[]{:S(2)}) async-start(bf16[16,128,128]{2,1,0:T(8,128)(2,1)} %apply.1), calls=%async_computation.2 | async-start | bytes 1048576 | tf_op jit(solution)/shard_map/all_to_all | solution.py:486
  80.2 0.0 collective-permute-start.2
  80.2 8.8 %middle.1 = (bf16[128,2048]{1,0:T(8,128)(2,1)}, f32[16,128,128]{2,1,0:T(8,128)}, f32[16,128,128]{2,1,0:T(8,128)}, f32[16,128,128]{2,1,0:T(8,128)}, f32[16,128,12...) custom-call(bf16[128,128]{1,0:T(8,128)(2,1)} %copy-done.6, ...), custom_call_target="tpu_custom_call" | custom-call | flops 4000000000 | bytes 12582912 | tf_op jit(solution)/shard_map/middle/pallas_call | solution.py:471
  89.0 5.1 %all-to-all-done.2.end_ref = bf16[16,128,128]{2,1,0:T(8,128)(2,1)S(1)} async-done(((bf16[16,128,128]{2,1,0:T(8,128)(2,1)}), bf16[16,128,128]{2,1,0:T(8,128)(2,1)S(1)}, u32[]{:S(2)}, u32[]{:S(2)}) %all-to-all-start.2) | async-done | bytes 524320 | tf_op jit(solution)/shard_map/all_to_all | solution.py:486
  94.1 0.8 copy-done.17
  94.9 10.1 %second.1 = (bf16[128,2048]{1,0:T(8,128)(2,1)}, bf16[128,2048]{1,0:T(8,128)(2,1)}, bf16[1232,128]{1,0:T(8,128)(2,1)}, bf16[1232,128]{1,0:T(8,128)(2,1)}, bf16[12...) custom-call(s32[1]{0:T(128)} %bitcast.core_ref, bf16[16,128,128]{2,1,0:T(8,128)(2,1)} %copy-done.4, f32[128,16]{1,0:T(8,128)} %copy-done.10, ...), custom_call_target="tpu_custom_call" | custom-call | flops 4000000000 | bytes 12582912 | tf_op jit(solution)/shard_map/second/pallas_call | solution.py:494
  105.0 0.1 collective-permute-start.4
  105.1 0.0 copy-done.7
  105.1 0.5 collective-permute-start.3
  105.6 0.0 collective-permute-done.2.hid2_ref
  105.6 1.4 collective-permute-done.3.rank2_ref
  107.0 0.0 collective-permute-done.4.got_ref
  107.0 1.0 copy-done.5
  107.9 0.6 terms.1
  108.5 0.0 copy-start.9
  108.5 13.8 %all_to_all.32.in_ref = bf16[4,624,128]{2,1,0:T(8,128)(2,1)S(1)} all-to-all(bf16[4,624,128]{2,1,0:T(8,128)(2,1)S(1)} %terms.1), channel_id=1, replica_groups=mesh['x'=4,'core'=2,'y'=2,'z'=16] {'x'}, dimensions={0} | all-to-all | bytes 1277952 | tf_op jit(solution)/shard_map/all_to_all | solution.py:512
  122.4 0.8 total.1
  123.1 5.4 %all-to-all-start.4 = ((bf16[32,24,128]{2,1,0:T(8,128)(2,1)}), bf16[32,24,128]{2,1,0:T(8,128)(2,1)S(1)}, u32[]{:S(2)}, u32[]{:S(2)}) async-start(bf16[32,24,128]{2,1,0:T(8,128)(2,1)} %bitcast.20), calls=%async_computation.4 | async-start | bytes 393216 | tf_op jit(solution)/shard_map/all_to_all | solution.py:516
  128.6 0.0 copy-done.9
  128.6 0.0 copy-start.18
  128.6 0.1 reshape.77
  128.7 10.2 %all-to-all-done.4.in_ref = bf16[32,24,128]{2,1,0:T(8,128)(2,1)S(1)} async-done(((bf16[32,24,128]{2,1,0:T(8,128)(2,1)}), bf16[32,24,128]{2,1,0:T(8,128)(2,1)S(1)}, u32[]{:S(2)}, u32[]{:S(2)}) %all-to-all-start.4) | async-done | bytes 196640 | tf_op jit(solution)/shard_map/all_to_all | solution.py:516
  139.0 0.7 share.1
  139.7 4.5 %all-to-all-start.5 = ((bf16[32,24,128]{2,1,0:T(8,128)(2,1)}), bf16[32,24,128]{2,1,0:T(8,128)(2,1)S(1)}, u32[]{:S(2)}, u32[]{:S(2)}) async-start(bf16[32,24,128]{2,1,0:T(8,128)(2,1)} %share.1), calls=%async_computation.5 | async-start | bytes 393216 | tf_op jit(solution)/shard_map/all_to_all | solution.py:518
  144.2 0.0 copy-done.19
  144.2 0.3 fusion.2
  144.5 0.0 copy-done.18
  144.5 1.1 fusion.1
  145.7 9.0 %all-to-all-done.5 = bf16[32,24,128]{2,1,0:T(8,128)(2,1)S(1)} async-done(((bf16[32,24,128]{2,1,0:T(8,128)(2,1)}), bf16[32,24,128]{2,1,0:T(8,128)(2,1)S(1)}, u32[]{:S(2)}, u32[]{:S(2)}) %all-to-all-start.5) | async-done | bytes 196640 | tf_op jit(solution)/shard_map/all_to_all | solution.py:518
  154.7 0.7 unpack.1
  (11 shorter events, 0.0 us)
Async XLA Ops:
  0.6 16.5 %copy-start = (bf16[1,128,2304]{2,1,0:T(8,128)(2,1)S(1)}, bf16[1,128,2304]{2,1,0:T(8,128)(2,1)}, u32[]{:S(2)}) copy-start(bf16[1,128,2304]{2,1,0:T(8,128)(2,1)} %param.11) | copy-start | bytes 1769476
  17.1 2.0 %collective-permute-start = (bf16[4,592,128]{2,1,0:T(8,128)(2,1)S(1)}, bf16[4,592,128]{2,1,0:T(8,128)(2,1)S(1)}, u32[]{:S(2)}, u32[]{:S(2)}) collective-permute-start(bf16[4,592,128]{2,1,0:T(8,128)(2,1)S(1)} %all_to_all.30.ours_ref), channel_id=1, source_target_pairs={{0,32},{32,0},{1,33},{33,1},{2,34},{34,2},{3,35},{35,3},{4,36},{36... | collective-permute-start | bytes 1818632 | tf_op jit(solution)/shard_map/ppermute | solution.py:433
  19.2 1.0 copy-start.1
  19.2 1.2 copy-start.2
  19.2 1.4 copy-start.3
  19.2 1.4 copy-start.11
  19.2 1.4 copy-start.12
  19.8 8.1 %copy-start.8 = (bf16[8,48,128]{2,1,0:T(8,128)(2,1)}, bf16[8,48,128]{2,1,0:T(8,128)(2,1)S(1)}, u32[]{:S(2)}) copy-start(bf16[8,48,128]{2,1,0:T(8,128)(2,1)S(1)} %get-tuple-element.65) | copy-start | bytes 294916
  19.8 8.1 %copy-start.10 = (f32[128,16]{1,0:T(8,128)}, f32[128,16]{1,0:T(8,128)S(1)}, u32[]{:S(2)}) copy-start(f32[128,16]{1,0:T(8,128)S(1)} %get-tuple-element.43.beta_ref) | copy-start | bytes 24580
  19.9 45.4 %copy-start.4 = (bf16[16,128,128]{2,1,0:T(8,128)(2,1)}, bf16[16,128,128]{2,1,0:T(8,128)(2,1)S(1)}, u32[]{:S(2)}) copy-start(bf16[16,128,128]{2,1,0:T(8,128)(2,1)S(1)} %get-tuple-element.42.up_ref) | copy-start | bytes 1572868
  19.9 45.4 %copy-start.6 = (bf16[128,128]{1,0:T(8,128)(2,1)}, bf16[128,128]{1,0:T(8,128)(2,1)S(1)}, u32[]{:S(2)}) copy-start(bf16[128,128]{1,0:T(8,128)(2,1)S(1)} %get-tuple-element.41.low_ref.rank_ref) | copy-start | bytes 98308
  28.0 1.0 copy-start.13
  29.0 37.9 %copy-start.14 = (f32[16,128,128]{2,1,0:T(8,128)}, f32[16,128,128]{2,1,0:T(8,128)S(1)}, u32[]{:S(2)}) copy-start(f32[16,128,128]{2,1,0:T(8,128)S(1)} %get-tuple-element.52.mix_ref) | copy-start | bytes 3145732
  29.0 37.9 %copy-start.15 = (f32[16,128,128]{2,1,0:T(8,128)}, f32[16,128,128]{2,1,0:T(8,128)S(1)}, u32[]{:S(2)}) copy-start(f32[16,128,128]{2,1,0:T(8,128)S(1)} %get-tuple-element.46.cum_ref) | copy-start | bytes 3145732
  29.0 37.9 %copy-start.16 = (f32[16,128,128]{2,1,0:T(8,128)}, f32[16,128,128]{2,1,0:T(8,128)S(1)}, u32[]{:S(2)}) copy-start(f32[16,128,128]{2,1,0:T(8,128)S(1)} %get-tuple-element.45.sco_ref) | copy-start | bytes 3145732
  66.9 7.3 %collective-permute-start.1 = (bf16[128,128]{1,0:T(8,128)(2,1)S(1)}, bf16[128,128]{1,0:T(8,128)(2,1)S(1)}, u32[]{:S(2)}, u32[]{:S(2)}) collective-permute-start(bf16[128,128]{1,0:T(8,128)(2,1)S(1)} %get-tuple-element.51), channel_id=1, source_target_pairs={{16,0},{17,1},{18,2},{19,3},{20,4},{21,5},{22,6},{23,7},{24,8},{25... | collective-permute-start | bytes 98312 | tf_op jit(solution)/shard_map/ppermute | solution.py:484
  75.3 18.8 %all-to-all-start.2 = ((bf16[16,128,128]{2,1,0:T(8,128)(2,1)}), bf16[16,128,128]{2,1,0:T(8,128)(2,1)S(1)}, u32[]{:S(2)}, u32[]{:S(2)}) async-start(bf16[16,128,128]{2,1,0:T(8,128)(2,1)} %apply.1), calls=%async_computation.2 | async-start | bytes 1048576 | tf_op jit(solution)/shard_map/all_to_all | solution.py:486
  80.2 25.4 %collective-permute-start.2 = (bf16[2304,128]{1,0:T(8,128)(2,1)S(1)}, bf16[2304,128]{1,0:T(8,128)(2,1)S(1)}, u32[]{:S(2)}, u32[]{:S(2)}) collective-permute-start(bf16[2304,128]{1,0:T(8,128)(2,1)S(1)} %bitcast.35), channel_id=1, source_target_pairs={{0,32},{32,0},{1,33},{33,1},{2,34},{34,2},{3,35},{35,3},{4,36},{36... | collective-permute-start | bytes 1769480 | tf_op jit(solution)/shard_map/ppermute | solution.py:489
  94.1 0.8 copy-start.17
  94.9 10.2 %copy-start.7 = (bf16[128,128]{1,0:T(8,128)(2,1)S(1)}, bf16[128,128]{1,0:T(8,128)(2,1)}, u32[]{:S(2)}) copy-start(bf16[128,128]{1,0:T(8,128)(2,1)} %copy-done.6) | copy-start | bytes 98308
  105.0 2.0 %collective-permute-start.4 = (bf16[1232,128]{1,0:T(8,128)(2,1)}, bf16[1232,128]{1,0:T(8,128)(2,1)S(1)}, u32[]{:S(2)}, u32[]{:S(2)}) collective-permute-start(bf16[1232,128]{1,0:T(8,128)(2,1)} %get-tuple-element.67), channel_id=1, source_target_pairs={{0,32},{32,0},{1,33},{33,1},{2,34},{34,2},{3,35},{35,3},{4,36},{36... | collective-permute-start | bytes 946184 | tf_op jit(solution)/shard_map/ppermute | solution.py:505
  105.1 1.8 %collective-permute-start.3 = (bf16[128,128]{1,0:T(8,128)(2,1)S(1)}, bf16[128,128]{1,0:T(8,128)(2,1)S(1)}, u32[]{:S(2)}, u32[]{:S(2)}) collective-permute-start(bf16[128,128]{1,0:T(8,128)(2,1)S(1)} %copy-done.7), channel_id=1, source_target_pairs={{0,32},{32,0},{1,33},{33,1},{2,34},{34,2},{3,35},{35,3},{4,36},{36... | collective-permute-start | bytes 98312 | tf_op jit(solution)/shard_map/ppermute | solution.py:490
  107.0 1.0 copy-start.5
  108.5 20.0 %copy-start.9 = (bf16[8,48,128]{2,1,0:T(8,128)(2,1)S(1)}, bf16[8,48,128]{2,1,0:T(8,128)(2,1)}, u32[]{:S(2)}) copy-start(bf16[8,48,128]{2,1,0:T(8,128)(2,1)} %copy-done.8) | copy-start | bytes 294916
  122.4 21.8 %copy-start.19 = (bf16[16,128]{1,0:T(8,128)(2,1)S(1)}, bf16[16,128]{1,0:T(8,128)(2,1)}, u32[]{:S(2)}) copy-start(bf16[16,128]{1,0:T(8,128)(2,1)} %get-tuple-element.64) | copy-start | bytes 12292
  123.1 15.8 %all-to-all-start.4 = ((bf16[32,24,128]{2,1,0:T(8,128)(2,1)}), bf16[32,24,128]{2,1,0:T(8,128)(2,1)S(1)}, u32[]{:S(2)}, u32[]{:S(2)}) async-start(bf16[32,24,128]{2,1,0:T(8,128)(2,1)} %bitcast.20), calls=%async_computation.4 | async-start | bytes 393216 | tf_op jit(solution)/shard_map/all_to_all | solution.py:516
  128.6 16.0 %copy-start.18 = (bf16[128,128]{1,0:T(8,128)(2,1)S(1)}, bf16[128,128]{1,0:T(8,128)(2,1)}, u32[]{:S(2)}) copy-start(bf16[128,128]{1,0:T(8,128)(2,1)} %get-tuple-element.62) | copy-start | bytes 98308
  139.7 15.0 %all-to-all-start.5 = ((bf16[32,24,128]{2,1,0:T(8,128)(2,1)}), bf16[32,24,128]{2,1,0:T(8,128)(2,1)S(1)}, u32[]{:S(2)}, u32[]{:S(2)}) async-start(bf16[32,24,128]{2,1,0:T(8,128)(2,1)} %share.1), calls=%async_computation.5 | async-start | bytes 393216 | tf_op jit(solution)/shard_map/all_to_all | solution.py:518
